TPU v7x, 512 devices: a whole 4x8x8 slice. The times are simulated.
512 devices in a mesh: dp: 32 (over y, x), seq: 16 (over z, core).
Axes of the slice: x: 4, y: 8, z: 8, core: 2. Of those that a mesh axis runs over, the one named last changes fastest.
Arguments:
- token_input: bfloat16 [32, 2048, 4096], P('dp', 'seq')
- input_map: bfloat16 [32, 2048, 128], P('dp', 'seq'), may hold values from -6 to 6
- output_map: bfloat16 [32, 2048, 128], P('dp', 'seq'), may hold values from -6 to 6
- step_size: float32 [32, 2048, 64], P('dp', 'seq'), may hold values from 0.005 to 0.1
- forget: float32 [32, 2048, 64], P('dp', 'seq'), as said below
- skip_gain: float32 [64], replicated, may hold values from 0.5 to 2
- segments: int32 [32, 16, 128], P('dp', 'seq'), may hold values from 0 to 7, never falling along the last dimension, each value on 1 to 32 neighbouring positions
- yield_rank: int32 [32, 128], P('dp'), may hold values from 0 to 63
- pair_mask: int32 [32, 128, 128], P('dp', 'seq'), may hold values from 0 to 1, as said below
- comparator: bfloat16 [4096, 64], replicated, may hold values from -0.01171875 to 0.01171875
Outputs:
- list_loss: float32 [32], P('dp')
- pooled_grad: float32 [32, 128, 4096], P('dp', 'seq')
- weight_grad: float32 [4096, 64], P(('dp', 'seq'))
Inputs may be any that keep to these rules, and one draw needn't show every extreme that they name: `segments`: within each block the numbers never fall and every number of 0 to 7 occurs. pair_mask[g, i, j] equals pair_mask[g, j, i], and pair_mask[g, i, i] is 0. `forget`: Positive.
All inputs are finite; a program needn't handle non-finite values.
Results may differ from a plain program's by a relative error of at most 0.011.
Values may be sent and summed in bfloat16 or wider, within the bound.
A program may use at most 128 MiB of HBM per device.

v0:
```python
import jax
import jax.numpy as jnp
from jax import lax
from jax.sharding import PartitionSpec as P

full_precision = lax.Precision.HIGHEST
norm_epsilon = 1e-05


def prefix(value, axis, join, neutral):
    count, mine = (lax.axis_size(axis), lax.axis_index(axis))
    pieces = jax.tree.map(lambda part: lax.all_gather(part, axis), value)
    so_far = jax.tree.map(
        lambda part, zero: jnp.full_like(part, 0) + jnp.asarray(zero, part.dtype), value, neutral
    )

    def hop(position, so_far):
        longer = join(so_far, jax.tree.map(lambda part: part[position], pieces))
        return jax.tree.map(lambda new, old: jnp.where(position < mine, new, old), longer, so_far)

    return lax.fori_loop(0, count - 1, hop, so_far)


def local_block(token_input, input_map, output_map, step_size, forget):
    length, inner_width = token_input.shape
    head_count = step_size.shape[1]
    head_width = inner_width // head_count
    decay_log = jnp.cumsum(-forget, axis=0)
    block_total = decay_log[-1]
    scores = lax.dot_general(
        output_map, input_map, (((1,), (1,)), ((), ())), preferred_element_type=jnp.float32
    )
    causal = lax.broadcasted_iota(jnp.int32, (length, length), 0) >= lax.broadcasted_iota(
        jnp.int32, (length, length), 1
    )
    group_outputs = []
    for group_index in range(head_count // 8):
        first_head = group_index * 8
        decay_part = decay_log[:, first_head : first_head + 8].T
        step_part = step_size[:, first_head : first_head + 8].T
        spacing = jnp.where(causal[None], decay_part[:, :, None] - decay_part[:, None, :], -jnp.inf)
        mixing = (scores[None] * jnp.exp(spacing) * step_part[:, None, :]).astype(jnp.bfloat16)
        group_values = token_input[
            :, first_head * head_width : (first_head + 8) * head_width
        ].reshape(length, 8, head_width)
        group_outputs.append(
            jnp.einsum("gts,sgp->tgp", mixing, group_values, preferred_element_type=jnp.float32)
        )
    local_out = jnp.concatenate(group_outputs, axis=1)
    token_heads = token_input.reshape(length, head_count, head_width)
    end_weight = jnp.exp(block_total[None, :] - decay_log) * step_size
    scaled = (
        (token_heads * end_weight[:, :, None]).astype(jnp.bfloat16).reshape(length, inner_width)
    )
    block_state = lax.dot_general(
        scaled, input_map, (((0,), (0,)), ((), ())), preferred_element_type=jnp.float32
    )
    return (
        local_out,
        decay_log,
        jnp.exp(block_total),
        block_state.reshape(head_count, head_width, -1),
    )


def compose(earlier, later):
    return (earlier[0] * later[0], later[0][:, None, None] * earlier[1] + later[1])


def pool_rows(layer_output, labels, nearby_candidate):
    length, head_count, head_width = layer_output.shape
    membership = (
        labels[None, :] == lax.broadcasted_iota(jnp.int32, (nearby_candidate, 1), 0)
    ).astype(jnp.float32)
    segment_sums = jnp.dot(
        membership, layer_output.reshape(length, head_count * head_width), precision=full_precision
    )
    segment_counts = jnp.sum(membership, axis=1)
    segment_means = (segment_sums / segment_counts[:, None]).reshape(
        nearby_candidate, head_count, head_width
    )
    normalized = segment_means / jnp.sqrt(
        jnp.mean(segment_means * segment_means, axis=2, keepdims=True) + norm_epsilon
    )
    return normalized.reshape(nearby_candidate, head_count * head_width).astype(jnp.bfloat16)


def per_device(
    token_input,
    input_map,
    output_map,
    step_size,
    forget,
    skip_gain,
    segments,
    yield_rank,
    pair_mask,
    comparator,
):
    tokens = token_input[0]
    length, inner_width = tokens.shape
    head_count = step_size.shape[2]
    head_width = inner_width // head_count
    nearby_candidate = pair_mask.shape[1]
    out_block = output_map[0]
    local_out, decay_log, block_decay, block_state = local_block(
        tokens, input_map[0], out_block, step_size[0], forget[0]
    )
    identity = (jnp.ones_like(block_decay), jnp.zeros_like(block_state))
    incoming = prefix((block_decay, block_state), "seq", compose, identity)[1]
    carried_low = incoming.astype(jnp.bfloat16).reshape(inner_width, -1)
    from_past = lax.dot_general(
        out_block, carried_low, (((1,), (1,)), ((), ())), preferred_element_type=jnp.float32
    ).reshape(length, head_count, head_width)
    token_heads = tokens.reshape(length, head_count, head_width)
    layer_output = (
        local_out
        + from_past * jnp.exp(decay_log)[:, :, None]
        + skip_gain[None, :, None] * token_heads
    )
    pooled = pool_rows(layer_output, segments[0, 0], nearby_candidate)
    all_pooled = lax.all_gather(pooled, "seq", axis=0, tiled=True)
    cand_count = all_pooled.shape[0]
    head_weight = comparator.reshape(head_count, head_width, head_width)
    skewed = (
        jnp.swapaxes(head_weight, 1, 2).astype(jnp.float32) - head_weight.astype(jnp.float32)
    ).astype(jnp.bfloat16)
    own_heads = pooled.reshape(nearby_candidate, head_count, head_width)
    all_heads = all_pooled.reshape(cand_count, head_count, head_width)
    own_projected = (
        jnp.einsum("cha,hab->chb", own_heads, head_weight, preferred_element_type=jnp.float32)
        .astype(jnp.bfloat16)
        .reshape(nearby_candidate, inner_width)
    )
    all_projected = (
        jnp.einsum("cha,hab->chb", all_heads, head_weight, preferred_element_type=jnp.float32)
        .astype(jnp.bfloat16)
        .reshape(cand_count, inner_width)
    )
    contract_last = (((1,), (1,)), ((), ()))
    score_rows = lax.dot_general(
        own_projected, all_pooled, contract_last, preferred_element_type=jnp.float32
    )
    score_columns = lax.dot_general(
        pooled, all_projected, contract_last, preferred_element_type=jnp.float32
    )
    margin = score_rows - score_columns
    seq_index = lax.axis_index("seq")
    own_rank = lax.dynamic_slice_in_dim(
        yield_rank[0], seq_index * nearby_candidate, nearby_candidate
    )
    other_rank = yield_rank[0]
    target = jnp.where(
        own_rank[:, None] < other_rank[None, :],
        1.0,
        jnp.where(own_rank[:, None] > other_rank[None, :], 0.0, 0.5),
    ).astype(jnp.float32)
    valid_pairs = pair_mask[0].astype(jnp.float32)
    pair_loss = jnp.sum(valid_pairs * (jax.nn.softplus(margin) - target * margin)) / (
        cand_count * cand_count
    )
    list_loss = lax.psum(pair_loss, "seq").reshape(1)
    pair_grad = (2.0 * valid_pairs * (jax.nn.sigmoid(margin) - target)).astype(jnp.bfloat16)
    all_skew = (
        jnp.einsum("cha,hab->chb", all_heads, skewed, preferred_element_type=jnp.float32)
        .astype(jnp.bfloat16)
        .reshape(cand_count, inner_width)
    )
    pooled_grad = jnp.dot(pair_grad, all_skew, preferred_element_type=jnp.float32)
    accumulated = jnp.dot(pair_grad, all_pooled, preferred_element_type=jnp.float32).reshape(
        nearby_candidate, head_count, head_width
    )
    weight_part = jnp.einsum(
        "cha,chb->hab", own_heads.astype(jnp.float32), accumulated, precision=full_precision
    )
    weight_part = (weight_part / (cand_count * lax.axis_size("dp"))).reshape(
        inner_width, head_width
    )
    weight_grad = lax.psum_scatter(weight_part, ("dp", "seq"), scatter_dimension=0, tiled=True)
    return (list_loss, pooled_grad.reshape(1, nearby_candidate, inner_width), weight_grad)


def solution(mesh):
    return jax.shard_map(
        per_device,
        mesh=mesh,
        in_specs=(
            P("dp", "seq", None),
            P("dp", "seq", None),
            P("dp", "seq", None),
            P("dp", "seq", None),
            P("dp", "seq", None),
            P(),
            P("dp", "seq", None),
            P("dp", None),
            P("dp", "seq", None),
            P(),
        ),
        out_specs=(P("dp"), P("dp", "seq", None), P(("dp", "seq"), None)),
        check_vma=False,
    )
```

profile of v0, /device:TPU:1, one launch (start us, length us, event | category | flops | bytes accessed | tf_op | source)
XLA Modules:
  0.0 565.3 jit_solution(10189890765324635350)
XLA Ops:
  34.9 24.6 %all-gather.1 = f32[16,1,64]{2,1,0:T(1,128)S(1)} all-gather(f32[1,1,64]{2,1,0:T(1,128)} %get-tuple-element.137), channel_id=1, replica_groups=mesh['dp'=32,'seq'=16] {'seq'}, dimensions={0}, use_global_device_ids=true | all-gather | bytes 4352 | tf_op jit(solution)/shard_map/all_gather | solution.py:12
  70.6 125.9 %all-gather.7.cloned.1.call-done = f32[1024,64,128]{2,1,0:T(8,128)} async-done(((f32[64,64,128]{2,1,0:T(8,128)}), f32[1024,64,128]{2,1,0:T(8,128)}) %all-gather.7.cloned.1.call-update) | async-done | bytes 33554448 | tf_op jit(solution)/shard_map/all_gather | solution.py:12
  196.5 31.8 %while.14 = (s32[]{:T(128)}, f32[64,64,128]{2,1,0:T(8,128)S(1)}, s32[]{:T(128)}, f32[16,64]{1,0:T(8,128)S(1)}, f32[16,64,64,128]{3,2,1,0:T(8,128)}, /*index=5*/s32[]{:T(128)}, s32[]{:T(128)}) while((s32[]{:T(128)}, f32[64,64,128]{2,1,0:T(8,128)S(1)}, s32[]{:T(128)}, f32[16,64]{1,0:T(8,128)S(1)}, f32[16,64,64,128]{3,2,1,0:T(8,128)}, ...), condition=%wide.region_2.3_spmd.clone, body=%wide.region_1.2_spmd.clone.sunk | while | flops 2097156 | bytes 6292329 | solution.py:21
  198.7 2.1 fusion.116
  200.8 2.1 fusion.116
  202.9 2.1 fusion.116
  205.0 2.1 fusion.116
  207.2 2.1 fusion.116
  209.3 2.1 fusion.116
  211.4 2.1 fusion.116
  213.5 2.1 fusion.116
  215.6 2.1 fusion.116
  217.8 2.1 fusion.116
  219.9 2.1 fusion.116
  222.0 2.1 fusion.116
  224.1 2.1 fusion.116
  226.3 2.1 fusion.116
  228.7 2.2 fusion.3
  236.9 36.5 %all-gather.5.cloned.1.call-done = bf16[128,4096]{1,0:T(8,128)(2,1)} async-done(((bf16[8,4096]{1,0:T(8,128)(2,1)}), bf16[128,4096]{1,0:T(8,128)(2,1)}) %all-gather.5.cloned.1.call-update) | async-done | bytes 1048592 | tf_op jit(solution)/shard_map/all_gather | solution.py:122
  277.8 2.3 convolution_multiply_fusion
  282.1 3.0 copy.169
  285.8 24.9 %psum.7 = f32[1]{0:T(128)} all-reduce(f32[1]{0:T(128)} %bitcast.57), channel_id=1, replica_groups=mesh['dp'=32,'seq'=16] {'seq'}, use_global_device_ids=true, to_apply=%region_6.7 | all-reduce | flops 1 | bytes 8 | tf_op jit(solution)/shard_map/psum | solution.py:162
  310.7 2.7 convolution_convert_fusion.1
  314.4 243.0 %all-reduce.3.cloned.1.call-done = f32[4096,64]{1,0:T(8,128)} async-done(((f32[4096,64]{1,0:T(8,128)}), f32[4096,64]{1,0:T(8,128)}) %all-reduce.3.cloned.1.call-update) | async-done | bytes 1048592
  (140 shorter events, 55.7 us)
Async XLA Ops:
  7.2 3.7 copy-start
  7.2 1.8 copy-start.6
  7.2 189.3 %all-gather.7.cloned.1.call-start = ((), (), s32[]{:S(2)}) async-start(), calls=%async_computation.1 | async-start | bytes 35651584 | tf_op jit(solution)/shard_map/all_gather | solution.py:12
  12.6 22.2 %copy-start.22 = (f32[64]{0:T(128)S(1)}, f32[64]{0:T(128)}, u32[]{:S(2)}) copy-start(f32[64]{0:T(128)} %param.17) | copy-start | bytes 772
  12.6 48.3 %copy-start.5 = (bf16[1,128,128]{2,1,0:T(8,128)(2,1)S(1)}, bf16[1,128,128]{2,1,0:T(8,128)(2,1)}, u32[]{:S(2)}) copy-start(bf16[1,128,128]{2,1,0:T(8,128)(2,1)} %param.14) | copy-start | bytes 98308
  12.6 260.7 %all-gather.5.cloned.1.call-start = ((), (), s32[]{:S(2)}) async-start(), calls=%async_computation | async-start | bytes 1114112 | tf_op jit(solution)/shard_map/all_gather | solution.py:122
  34.9 26.2 %copy-start.20 = (f32[8,128]{1,0:T(8,128)S(1)}, f32[8,128]{1,0:T(8,128)}, u32[]{:S(2)}) copy-start(f32[8,128]{1,0:T(8,128)} %copy.138) | copy-start | bytes 12292
  61.0 3.1 copy-start.17
  61.0 3.1 copy-start.19
  61.1 4.0 copy-start.15
  61.1 4.0 copy-start.18
  61.2 5.1 copy-start.13
  61.2 5.1 copy-start.16
  62.3 5.1 copy-start.10
  62.3 5.1 copy-start.14
  64.1 4.3 copy-start.9
  64.1 4.3 copy-start.11
  65.2 4.3 copy-start.12
  228.7 2.2 copy-start.21
  228.7 2.2 copy-start.24
  230.9 2.6 copy-start.4
  232.0 2.7 copy-start.23
  233.3 324.2 %all-reduce.3.cloned.1.call-start = ((), (), s32[]{:S(2)}) async-start(), calls=%async_computation.2 | async-start | bytes 4194304
  285.8 273.0 %copy-start.1 = (bf16[1,128,128]{2,1,0:T(8,128)(2,1)S(1)}, bf16[1,128,128]{2,1,0:T(8,128)(2,1)}, u32[]{:S(2)}) copy-start(bf16[1,128,128]{2,1,0:T(8,128)(2,1)} %param.13) | copy-start | bytes 98308
  (4 other events, 6.1 us)
Sparse Core Ops, SparseCore 0:
  12.7 183.7 all-gather.6
  233.4 39.8 all-gather.4
  280.3 277.1 all-reduce.2
where the time goes:
time: 567 us; the launch traced here: 565 us
  waiting for transfers between devices  406 us (72%)
  blocking collectives  49.5 us (9%)
  other arithmetic  36.6 us (6%)
  local copies, waits for them, and re-layouts  34.2 us (6%)
  matrix products  23.8 us (4%)
  between operations  14.8 us (3%)
    unnamed x4, waiting for transfers between devices  243 us
    all_gather x1, waiting for transfers between devices, prefix(): pieces = jax.tree.map(lambda part: lax.all_gather(part, axis), value)  126 us
    all_gather x1, waiting for transfers between devices, per_device(): all_pooled = lax.all_gather(pooled, 'seq', axis=0, tiled=True)  36.5 us
    select_n x15, other arithmetic, hop(): jnp.where(position < mine, new, old)  31.2 us
    psum x1, blocking collectives, per_device(): list_loss = lax.psum(pair_loss, 'seq').reshape(1)  24.9 us
    all_gather x1, blocking collectives, prefix(): pieces = jax.tree.map(lambda part: lax.all_gather(part, axis), value)  24.6 us
    transpose x9, local copies, waits for them, and re-layouts, local_block(): step_part = step_size[:, first_head:first_head + 8].T  12.1 us
  transfers between devices with their start and end apart: 3, of which 3 were waited for; matrix products, arithmetic and copies ran while one was open for 8% of the time, Pallas kernels for 0%

commit v1 on v0

v1 whole, which is shorter than its diff:
```python
import jax
import jax.numpy as jnp
from jax import lax
from jax.experimental import pallas as pl
from jax.experimental.pallas import tpu as pltpu
from jax.sharding import PartitionSpec as P

HI = lax.Precision.HIGHEST
F32 = jnp.float32
BF16 = jnp.bfloat16
EPS = 1e-05
NS = 16
ND = 32
MESH = pl.DeviceIdType.MESH


def dot(a, b, precision=None):
    return lax.dot_general(
        a, b, (((1,), (0,)), ((), ())), precision=precision, preferred_element_type=F32
    )


def dot_t(a, b):
    return lax.dot_general(a, b, (((1,), (1,)), ((), ())), preferred_element_type=F32)


def iota(shape, axis):
    return lax.broadcasted_iota(jnp.int32, shape, axis)


def block_kernel(
    skip, tok, b_in, c_out, step, forget, seg, st_o, v_o, m_o, d_o, cols, dl_rows, step_rows
):
    lower = iota((128, 128), 0) >= iota((128, 128), 1)
    dl = -dot(lower.astype(F32), forget[...], HI)
    end_weight = jnp.exp(dl[127:128, :] - dl) * step[...]
    cols[...] = jnp.concatenate([dl, end_weight], axis=1)
    dl_rows[...] = jnp.transpose(dl)
    step_rows[...] = jnp.transpose(step[...])
    b_t = jnp.transpose(b_in[...].astype(F32)).astype(BF16)
    scores = jnp.where(lower, dot_t(c_out[...], b_in[...]), 0.0)
    member = (jnp.broadcast_to(seg[...], (8, 128)) == iota((8, 128), 0)).astype(F32)
    member_low = member.astype(BF16)
    inverse = 1.0 / jnp.sum(member, axis=1, keepdims=True)
    left = iota((128, 128), 1) < 64
    left8 = left[:8]
    left1 = left[:1]

    def group(j, _):
        query_rows = []
        totals = []
        for pair in range(2):
            lanes = pl.ds(pl.multiple_of(j * 256 + pair * 128, 128), 128)
            tokens = tok[:, lanes]
            mixed = []
            for i in range(2):
                at = pair * 2 + i
                row = dl_rows[pl.ds(j * 4 + at, 1), :]
                gap = cols[:, at : at + 1] - row
                mixing = scores * jnp.exp(jnp.minimum(gap, 0.0)) * step_rows[pl.ds(j * 4 + at, 1), :]
                mixed.append(dot(member_low, mixing.astype(BF16)) + skip[j * 4 + at] * member)
                past = jnp.exp(row)
                query_rows.append(member * inverse * past)
                totals.append(past[:, 127:128])
            both = dot(jnp.concatenate(mixed, axis=0).astype(BF16), tokens)
            m_o[j, :, pair * 128 : pair * 128 + 128] = (
                jnp.where(left8, both[:8], both[8:]) * inverse
            )
            base = 64 + pair * 2
            weight = jnp.where(left, cols[:, base : base + 1], cols[:, base + 1 : base + 2])
            scaled = (tokens.astype(F32) * weight).astype(BF16)
            st_o[j, :, pair * 128 : pair * 128 + 128] = dot(b_t, scaled).astype(BF16)
        v_o[j] = dot(jnp.concatenate(query_rows, axis=0).astype(BF16), c_out[...]).astype(BF16)
        first = jnp.where(left1, totals[0], totals[1])
        second = jnp.where(left1, totals[2], totals[3])
        d_o[j] = jnp.where(iota((8, 128), 0) == 0, first, second)
        cols[...] = pltpu.roll(cols[...], 124, 1)
        return 0

    lax.fori_loop(0, 16, group, 0)


def list_kernel(
    st, v, m, d, w_in, rank, mask,
    pg_o, loss_o, wg_o,
    r_st, r_v, r_m, r_d, carried, means, margin_part, r_margin, pair_own, r_pair, grad_part, r_grad,
    w_part, r_w,
    send_a, recv_a, own_a, send_b, recv_b, send_c, recv_c, send_d, recv_d, send_w, recv_w,
):
    me_d = lax.axis_index("dp")
    me = lax.axis_index("seq")
    home = me_d // 2

    def peer(k):
        return lax.rem(me + k, NS)

    barrier = pltpu.get_barrier_semaphore()

    def greet(k, _):
        pl.semaphore_signal(barrier, inc=1, device_id=(me_d, peer(k)), device_id_type=MESH)
        return 0

    lax.fori_loop(1, NS, greet, 0)

    def greet_source(s, _):
        @pl.when(jnp.logical_or(s != me_d, home != me))
        def _():
            pl.semaphore_signal(barrier, inc=1, device_id=(s, home), device_id_type=MESH)

        return 0

    lax.fori_loop(0, ND, greet_source, 0)
    pl.semaphore_wait(barrier, NS - 1 + ND - (home == me).astype(jnp.int32))

    def exchange(src, dst, send, recv, k):
        return pltpu.make_async_remote_copy(
            src_ref=src, dst_ref=dst, send_sem=send, recv_sem=recv,
            device_id=(me_d, peer(k)), device_id_type=MESH,
        )

    arrays = ((st, r_st), (v, r_v), (m, r_m), (d, r_d))

    def copies(k):
        return [
            exchange(src.at[peer(k)], dst.at[me], send_a.at[n, k], recv_a.at[n, k], k)
            for n, (src, dst) in enumerate(arrays)
        ]

    def start_a(k, _):
        for c in copies(k):
            c.start()
        return 0

    lax.fori_loop(1, NS, start_a, 0)
    own = [
        pltpu.make_async_copy(src.at[me], dst.at[me], own_a.at[n])
        for n, (src, dst) in enumerate(arrays)
    ]
    for c in own:
        c.start()
    wide = w_in[...].astype(F32)
    same = (iota((256, 256), 0) // 64) == (iota((256, 256), 1) // 64)
    blocks = jnp.where(same, jnp.concatenate([wide, wide, wide, wide], axis=1), 0.0)
    weight = blocks.astype(BF16)
    skewed = (jnp.transpose(blocks) - blocks).astype(BF16)
    for c in own:
        c.wait()

    def wait_a(k, _):
        for c in copies(k):
            c.wait()
        return 0

    lax.fori_loop(1, NS, wait_a, 0)

    carried[...] = jnp.zeros_like(carried)
    lane = iota((8, 256), 1) // 64

    def block(b, _):
        now = carried[...]
        past = dot(r_v[b], now.astype(BF16))
        total = r_m[b]
        for h in range(4):
            total = total + jnp.where(lane == h, past[h * 8 : h * 8 + 8], 0.0)
        means[pl.ds(pl.multiple_of(b * 8, 8), 8), :] = total
        decay = jnp.concatenate([r_d[b, 0:1, :], r_d[b, 1:2, :]], axis=1)
        carried[...] = decay * now + r_st[b].astype(F32)
        return 0

    lax.fori_loop(0, NS, block, 0)
    mean = means[...]
    square = dot(mean * mean, jnp.where(same, 1.0 / 64.0, 0.0), HI)
    pooled32 = mean / jnp.sqrt(square + EPS)
    pooled = pooled32.astype(BF16)
    projected = dot(pooled, weight).astype(BF16)
    margin_part[...] = dot_t(projected, pooled) - dot_t(pooled, projected)

    def margin_copy(k):
        rows = pl.ds(pl.multiple_of(peer(k) * 8, 8), 8)
        return exchange(margin_part.at[rows], r_margin.at[k], send_b.at[k], recv_b.at[k], k)

    def start_b(k, _):
        margin_copy(k).start()
        return 0

    lax.fori_loop(1, NS, start_b, 0)
    r_margin[0] = margin_part[pl.ds(pl.multiple_of(me * 8, 8), 8), :]
    skew_rows = dot(pooled, skewed).astype(BF16)
    pooled_t = jnp.transpose(pooled.astype(F32))
    ranks = jnp.broadcast_to(rank[...].astype(F32), (8, 128))
    mine = iota((8, 128), 1) == me * 8 + iota((8, 128), 0)
    own_rank = jnp.sum(jnp.where(mine, ranks, 0.0), axis=1, keepdims=True)
    target = jnp.where(own_rank < ranks, 1.0, jnp.where(own_rank > ranks, 0.0, 0.5))
    valid = mask[...].astype(F32)

    def wait_b(k, _):
        margin_copy(k).wait()
        return 0

    lax.fori_loop(1, NS, wait_b, 0)
    margin = jnp.sum(r_margin[...], axis=0)
    soft = jnp.maximum(margin, 0.0) + jnp.log(1.0 + jnp.exp(-jnp.abs(margin)))
    losses = jnp.sum(valid * (soft - target * margin), axis=0, keepdims=True)
    pair = 2.0 * valid * (1.0 / (1.0 + jnp.exp(-margin)) - target)
    sent = jnp.concatenate([pair, jnp.broadcast_to(losses, (8, 128))], axis=0)
    pair_own[...] = sent
    r_pair[me] = sent

    def pair_copy(k):
        return exchange(pair_own, r_pair.at[me], send_c.at[k], recv_c.at[k], k)

    def start_c(k, _):
        pair_copy(k).start()
        return 0

    lax.fori_loop(1, NS, start_c, 0)

    def wait_c(k, _):
        pair_copy(k).wait()
        return 0

    lax.fori_loop(1, NS, wait_c, 0)
    pairs = r_pair[...]
    all_pair = pairs[:, :8, :].reshape(128, 128).astype(BF16)
    accumulated = dot(all_pair, pooled)
    product = dot(pooled_t, accumulated, HI) * (1.0 / 4096.0)
    for h in range(4):
        rows = slice(h * 64, h * 64 + 64)
        w_part[rows, 0:64] = product[rows, h * 64 : h * 64 + 64]

    def w_copy(i):
        to_d = me * 2 + i // NS
        to_s = lax.rem(i, NS)
        return to_d, to_s, pltpu.make_async_remote_copy(
            src_ref=w_part.at[pl.ds(pl.multiple_of(i * 8, 8), 8)],
            dst_ref=r_w.at[me_d],
            send_sem=send_w.at[i], recv_sem=recv_w.at[me_d],
            device_id=(to_d, to_s), device_id_type=MESH,
        )

    def start_w(i, _):
        to_d, to_s, c = w_copy(i)
        itself = jnp.logical_and(to_d == me_d, to_s == me)

        @pl.when(jnp.logical_not(itself))
        def _():
            c.start()

        @pl.when(itself)
        def _():
            r_w[me_d] = w_part[pl.ds(pl.multiple_of(i * 8, 8), 8), :]

        return 0

    w_part[:, 64:128] = jnp.zeros((256, 64), F32)
    lax.fori_loop(0, 2 * NS, start_w, 0)
    grad_part[...] = dot(all_pair, skew_rows)

    def grad_copy(k):
        rows = pl.ds(pl.multiple_of(peer(k) * 8, 8), 8)
        return exchange(grad_part.at[rows], r_grad.at[me], send_d.at[k], recv_d.at[k], k)

    def start_d(k, _):
        grad_copy(k).start()
        return 0

    lax.fori_loop(1, NS, start_d, 0)
    r_grad[me] = grad_part[pl.ds(pl.multiple_of(me * 8, 8), 8), :]
    loss = jnp.sum(pairs[:, 8, :]) * (1.0 / (128.0 * 128.0))
    loss_o[...] = jnp.full((8, 128), loss, F32)

    def wait_d(k, _):
        grad_copy(k).wait()
        return 0

    lax.fori_loop(1, NS, wait_d, 0)
    for b in range(NS):
        pg_o[:, b * 256 : b * 256 + 256] = r_grad[b]

    def wait_w(i, _):
        to_d, to_s, c = w_copy(i)

        @pl.when(jnp.logical_not(jnp.logical_and(to_d == me_d, to_s == me)))
        def _():
            c.wait_send()

        arrived = pltpu.make_async_remote_copy(
            src_ref=w_part.at[pl.ds(0, 8)], dst_ref=r_w.at[i],
            send_sem=send_w.at[i], recv_sem=recv_w.at[i],
            device_id=(to_d, to_s), device_id_type=MESH,
        )

        @pl.when(jnp.logical_or(i != me_d, home != me))
        def _():
            arrived.wait_recv()

        return 0

    lax.fori_loop(0, ND, wait_w, 0)
    wg_o[...] = jnp.sum(r_w[...], axis=0)[:, :64]


def per_device(
    token_input, input_map, output_map, step_size, forget, skip_gain, segments, yield_rank,
    pair_mask, comparator,
):
    vmem = pl.BlockSpec(memory_space=pltpu.VMEM)
    shape = jax.ShapeDtypeStruct
    st, v, m, d = pl.pallas_call(
        block_kernel,
        out_shape=(
            shape((16, 128, 256), BF16),
            shape((16, 32, 128), BF16),
            shape((16, 8, 256), F32),
            shape((16, 8, 128), F32),
        ),
        in_specs=[pl.BlockSpec(memory_space=pltpu.SMEM)] + [vmem] * 6,
        out_specs=(vmem,) * 4,
        scratch_shapes=[
            pltpu.VMEM((128, 128), F32),
            pltpu.VMEM((64, 128), F32),
            pltpu.VMEM((64, 128), F32),
        ],
        name="block",
    )(
        skip_gain, token_input[0], input_map[0], output_map[0], step_size[0], forget[0],
        segments[0],
    )
    own_weight = lax.dynamic_slice_in_dim(comparator, lax.axis_index("seq") * 256, 256)
    sem = pltpu.SemaphoreType.DMA
    pooled_grad, loss, weight_grad = pl.pallas_call(
        list_kernel,
        out_shape=(shape((8, 4096), F32), shape((8, 128), F32), shape((8, 64), F32)),
        in_specs=[vmem] * 7,
        out_specs=(vmem,) * 3,
        scratch_shapes=[
            pltpu.VMEM((16, 128, 256), BF16),
            pltpu.VMEM((16, 32, 128), BF16),
            pltpu.VMEM((16, 8, 256), F32),
            pltpu.VMEM((16, 8, 128), F32),
            pltpu.VMEM((128, 256), F32),
            pltpu.VMEM((128, 256), F32),
            pltpu.VMEM((128, 128), F32),
            pltpu.VMEM((16, 8, 128), F32),
            pltpu.VMEM((16, 128), F32),
            pltpu.VMEM((16, 16, 128), F32),
            pltpu.VMEM((128, 256), F32),
            pltpu.VMEM((16, 8, 256), F32),
            pltpu.VMEM((256, 128), F32),
            pltpu.VMEM((32, 8, 128), F32),
            sem((4, 16)), sem((4, 16)), sem((4,)),
            sem((16,)), sem((16,)), sem((16,)), sem((16,)), sem((16,)), sem((16,)),
            sem((32,)), sem((32,)),
        ],
        compiler_params=pltpu.CompilerParams(collective_id=0, has_side_effects=True),
        name="list",
    )(st, v, m, d, own_weight, yield_rank, pair_mask[0])
    return (loss[0, :1], pooled_grad[None], weight_grad)


def solution(mesh):
    return jax.shard_map(
        per_device,
        mesh=mesh,
        in_specs=(
            P("dp", "seq", None),
            P("dp", "seq", None),
            P("dp", "seq", None),
            P("dp", "seq", None),
            P("dp", "seq", None),
            P(),
            P("dp", "seq", None),
            P("dp", None),
            P("dp", "seq", None),
            P(),
        ),
        out_specs=(P("dp"), P("dp", "seq", None), P(("dp", "seq"), None)),
        check_vma=False,
    )
```

time: 567 us -> 103 us (0.18)
  waiting for transfers between devices: 406 us -> 0 us
  Pallas kernels: 0 us -> 95.3 us
  blocking collectives: 49.5 us -> 0 us
  other arithmetic: 36.6 us -> 0 us
  local copies, waits for them, and re-layouts: 34.2 us -> 6.62 us
  matrix products: 23.8 us -> 0 us
  between operations: 14.8 us -> 0.66 us
    unnamed x4 -> x0, waiting for transfers between devices: 243 us -> none
    all_gather x2 -> x0, waiting for transfers between devices: 162 us -> none  [the longest x1 126 us: prefix(): pieces = jax.tree.map(lambda part: lax.all_gather(part, axis), value)]
    pallas_call x0 -> x2, Pallas kernels: none -> 95.3 us  [the longest x1 84.5 us: per_device(): pl.pallas_call(list_kernel, out_shape=(shape((8, 4096), F32), shape((8, 1...]
    select_n x15 -> x0, other arithmetic: 31.2 us -> none  [hop(): jnp.where(position < mine, new, old)]
    psum x1 -> x0, blocking collectives: 24.9 us -> none  [per_device(): list_loss = lax.psum(pair_loss, 'seq').reshape(1)]
    all_gather x1 -> x0, blocking collectives: 24.6 us -> none  [prefix(): pieces = jax.tree.map(lambda part: lax.all_gather(part, axis), value)]
    dot_general x20 -> x0, matrix products: 23.8 us -> none  [the longest x8 9.36 us: local_block(): jnp.einsum('gts,sgp->tgp', mixing, group_values, preferred_element_type=j...]
    transpose x18 -> x0, local copies, waits for them, and re-layouts: 21.2 us -> none  [the longest x9 12.1 us: local_block(): step_part = step_size[:, first_head:first_head + 8].T]
  transfers between devices with their start and end apart: 3 -> 0, of which waited for: 3 -> 0; matrix products, arithmetic and copies ran while one was open for 8% -> 0% of each run, Pallas kernels for 0% -> 0%
where the time goes in v1:
time: 103 us
  Pallas kernels  95.3 us (93%)
  local copies, waits for them, and re-layouts  6.62 us (6%)
    pallas_call x1, Pallas kernels, per_device(): pl.pallas_call(list_kernel, out_shape=(shape((8, 4096), F32), shape((8, 1...  84.5 us
    pallas_call x1, Pallas kernels, per_device(): pl.pallas_call(block_kernel, out_shape=(shape((16, 128, 256), BF16), shap...  10.8 us
    unnamed x13, local copies, waits for them, and re-layouts  5.43 us

profile of v1, /device:TPU:1, one launch (start us, length us, event | category | flops | bytes accessed | tf_op | source)
XLA Modules:
  0.0 102.6 jit_solution(4271405080489663772)
XLA Ops:
  0.6 0.0 copy-start
  0.6 1.0 %copy-done = bf16[4096,64]{0,1:T(8,128)(2,1)S(1)} copy-done((bf16[4096,64]{0,1:T(8,128)(2,1)S(1)}, bf16[4096,64]{0,1:T(8,128)(2,1)}, u32[]{:S(2)}) %copy-start) | copy-done | bytes 524312
  1.7 0.0 copy-start.1
  1.7 0.7 copy.16.w_in
  2.4 0.0 copy-done.1
  2.4 0.0 copy-start.2
  2.4 0.7 copy.13
  3.2 0.0 copy-done.2
  3.2 0.7 copy.14
  3.9 10.8 %block.1 = (bf16[16,128,256]{2,1,0:T(8,128)(2,1)}, bf16[16,32,128]{2,1,0:T(8,128)(2,1)}, f32[16,8,256]{2,1,0:T(8,128)}, f32[16,8,128]{2,1,0:T(8,128)}) custom-call(f32[64]{0:T(128)} %skip.1, bf16[128,4096]{1,0:T(8,128)(2,1)} %bitcast.9, bf16[128,128]{1,0:T(8,128)(2,1)} %bitcast.13, bf16[128,128]{1,0:T(8,128)(2,1)} %bitcast.14, f32[128,64]{1,0:T(8,128)} %bitcast.10, ...), custom_call_target="tpu_custom_call" | custom-call | tf_op jit(solution)/shard_map/block/pallas_call | solution.py:309
  14.8 84.5 %list.1 = (f32[8,4096]{1,0:T(8,128)}, f32[8,128]{1,0:T(8,128)}, f32[8,64]{1,0:T(8,128)}) custom-call(bf16[16,128,256]{2,1,0:T(8,128)(2,1)} %get-tuple-element.10.st, bf16[16,32,128]{2,1,0:T(8,128)(2,1)} %get-tuple-element.11.v, f32[16,8,256]{2,1,0:T(8,128)} %get-tuple-element.12.m, f32[16,8,128]{2,1,0:T(8,128)} %get-tuple-element.13.d, ...), custom_call_target="tpu_custom_call" | custom-call | tf_op jit(solution)/shard_map/list/pallas_call | solution.py:331
  99.2 1.2 %slice.3 = f32[1,1]{1,0:T(1,128)} slice(f32[8,128]{1,0:T(8,128)} %get-tuple-element.14), slice={[0:1], [0:1]} | slice | bytes 8 | tf_op jit(solution)/shard_map/slice | solution.py:358
  100.4 0.0 copy-start.3
  100.4 1.6 %copy.19 = f32[1,8,4096]{2,1,0:T(8,128)} copy(f32[1,8,4096]{2,1,0:T(8,128)} %bitcast.12) | data formatting | bytes 262144
  102.0 0.0 copy-done.3
  102.0 0.6 copy.20
  (1 shorter events, 0.0 us)
Async XLA Ops:
  0.6 1.0 %copy-start = (bf16[4096,64]{0,1:T(8,128)(2,1)S(1)}, bf16[4096,64]{0,1:T(8,128)(2,1)}, u32[]{:S(2)}) copy-start(bf16[4096,64]{0,1:T(8,128)(2,1)} %param.19) | copy-start | bytes 1572868
  1.7 0.8 copy-start.1
  2.4 0.8 copy-start.2
  100.4 1.6 %copy-start.3 = (f32[8,64]{1,0:T(8,128)S(1)}, f32[8,64]{1,0:T(8,128)}, u32[]{:S(2)}) copy-start(f32[8,64]{1,0:T(8,128)} %get-tuple-element.22) | copy-start | bytes 6148

commit v2 on v1

v2 whole, which is shorter than its diff:
```python
import jax
import jax.numpy as jnp
from jax import lax
from jax.experimental import pallas as pl
from jax.experimental.pallas import tpu as pltpu
from jax.sharding import PartitionSpec as P

HI = lax.Precision.HIGHEST
F32 = jnp.float32
BF16 = jnp.bfloat16
EPS = 1e-05
NS = 16
ND = 32
CHIPS = 8
AHEAD = 4
MESH = pl.DeviceIdType.MESH


def dot(a, b, precision=None):
    return lax.dot_general(
        a, b, (((1,), (0,)), ((), ())), precision=precision, preferred_element_type=F32
    )


def dot_t(a, b):
    return lax.dot_general(a, b, (((1,), (1,)), ((), ())), preferred_element_type=F32)


def iota(shape, axis):
    return lax.broadcasted_iota(jnp.int32, shape, axis)


def list_kernel(
    skip, tok, b_in, c_out, step, forget, seg, w_in, rank, mask,
    pg_o, loss_o, wg_o,
    cols, dl_rows, give_s, give_m, own_s, own_m, got_s, got_m, pack, r_pack, w_own,
    carried, means, margin_part, r_margin, pair_own, r_pair, grad_part, r_grad, w_part, r_w,
    send_g, recv_g, send_m, recv_m, send_a, recv_a, send_b, recv_b, send_c, recv_c,
    send_d, recv_d, send_w, recv_w, w_sem,
):
    me_d = lax.axis_index("dp")
    me = lax.axis_index("seq")
    chip = me // 2
    core = lax.rem(me, 2)
    home = me_d // 2

    def peer(k):
        return lax.rem(me + k, NS)

    barrier = pltpu.get_barrier_semaphore()

    def greet_source(s, _):
        @pl.when(jnp.logical_or(s != me_d, home != me))
        def _():
            pl.semaphore_signal(barrier, inc=1, device_id=(s, home), device_id_type=MESH)

        return 0

    lax.fori_loop(0, ND, greet_source, 0)

    def greet(k, _):
        pl.semaphore_signal(barrier, inc=1, device_id=(me_d, peer(k)), device_id_type=MESH)
        return 0

    lax.fori_loop(1, NS, greet, 0)
    w_fetch = pltpu.make_async_copy(
        w_in.at[:, pl.ds(pl.multiple_of(me * 256, 256), 256)], w_own, w_sem
    )
    w_fetch.start()

    upper = iota((128, 128), 0) <= iota((128, 128), 1)
    lower = iota((128, 128), 0) >= iota((128, 128), 1)
    dl = -dot(forget[...], upper.astype(F32), HI)
    end_weight = jnp.exp(dl[:, 127:128] - dl) * step[...]
    dl_rows[...] = dl
    cols[...] = jnp.transpose(jnp.concatenate([dl, end_weight], axis=0))
    b_t = jnp.transpose(b_in[...].astype(F32)).astype(BF16)
    scores = jnp.where(lower, dot_t(c_out[...], b_in[...]), 0.0)
    member = (jnp.broadcast_to(seg[...], (8, 128)) == iota((8, 128), 0)).astype(F32)
    member_low = member.astype(BF16)
    inverse = 1.0 / jnp.sum(member, axis=1, keepdims=True)
    average = member * inverse
    left = iota((128, 128), 1) < 64
    left8 = left[:8]

    def group(j, out_s, out_m, t):
        here = pltpu.roll(cols[...], lax.rem(128 - 4 * j, 128), 1)
        query_rows = []
        for pair in range(2):
            lanes = pl.ds(pl.multiple_of(j * 256 + pair * 128, 128), 128)
            at_lanes = slice(pair * 128, pair * 128 + 128)
            tokens = tok[:, lanes]
            mixed = []
            totals = []
            for i in range(2):
                at = pair * 2 + i
                row = dl_rows[pl.ds(j * 4 + at, 1), :]
                gap = here[:, at : at + 1] - row
                mixing = scores * jnp.exp(jnp.minimum(gap, 0.0)) * step[pl.ds(j * 4 + at, 1), :]
                mixed.append(dot(member_low, mixing.astype(BF16)) + skip[j * 4 + at] * member)
                past = jnp.exp(row)
                query_rows.append(average * past)
                totals.append(past[:, 127:128])
            both = dot(jnp.concatenate(mixed, axis=0).astype(BF16), tokens)
            out_m[t, 0:8, at_lanes] = jnp.where(left8, both[:8], both[8:]) * inverse
            out_m[t, 8:16, at_lanes] = jnp.where(left8, totals[0], totals[1])
            base = 64 + pair * 2
            weight = jnp.where(left, here[:, base : base + 1], here[:, base + 1 : base + 2])
            scaled = (tokens.astype(F32) * weight).astype(BF16)
            out_s[t, 0:128, at_lanes] = dot(b_t, scaled).astype(BF16)
        queries = dot(jnp.concatenate(query_rows, axis=0).astype(BF16), c_out[...]).astype(BF16)
        out_s[t, 128:160, 0:128] = queries
        out_s[t, 128:160, 128:256] = queries

    def target_chip(t):
        away = CHIPS // 2 + (t // 2 + lax.rem(t, 2)) * (1 - 2 * lax.rem(t, 2))
        return lax.rem(chip + away, CHIPS)

    def compute(t, _):
        to = target_chip(t) * 2
        group(to + 1 - core, give_s, give_m, t)
        group(to + core, own_s, own_m, t)
        return 0

    def give(t):
        other = (me_d, chip * 2 + 1 - core)
        return (
            pltpu.make_async_remote_copy(
                src_ref=give_s.at[t], dst_ref=got_s.at[t], send_sem=send_g.at[t],
                recv_sem=recv_g.at[t], device_id=other, device_id_type=MESH,
            ),
            pltpu.make_async_remote_copy(
                src_ref=give_m.at[t], dst_ref=got_m.at[t], send_sem=send_m.at[t],
                recv_sem=recv_m.at[t], device_id=other, device_id_type=MESH,
            ),
        )

    def send_give(t, _):
        for c in give(t):
            c.start()
        return 0

    lane = iota((8, 256), 1) // 64

    def by_head(rows):
        total = jnp.where(lane == 0, rows[0:8], 0.0)
        for h in range(1, 4):
            total = total + jnp.where(lane == h, rows[h * 8 : h * 8 + 8], 0.0)
        return total

    def combine(t, out, at):
        for c in give(t):
            c.wait()
        first = core == 0
        mine, theirs = own_s[t], got_s[t]
        early = jnp.where(first, mine, theirs)
        late = jnp.where(first, theirs, mine)
        mine_m, theirs_m = own_m[t], got_m[t]
        early_m = jnp.where(first, mine_m, theirs_m)
        late_m = jnp.where(first, theirs_m, mine_m)
        early_d, late_d = early_m[8:9, :], late_m[8:9, :]
        state = late_d * early[:128].astype(F32) + late[:128].astype(F32)
        late_q = late[128:160, 0:128]
        within = by_head(dot(late_q, early[:128]))
        scaled_q = late_q.astype(F32)
        scaled_q = jnp.concatenate(
            [scaled_q[h * 8 : h * 8 + 8] * early_d[:, h * 64 : h * 64 + 1] for h in range(4)],
            axis=0,
        )
        out[at, 0:128, :] = state.astype(BF16)
        out[at, 128:160, 0:128] = early[128:160, 0:128]
        out[at, 128:160, 128:256] = scaled_q.astype(BF16)
        out[at, 160:176, :] = jnp.concatenate(
            [early_m[0:8], late_m[0:8] + within], axis=0
        ).astype(BF16)
        decay = early_d * late_d
        high = decay.astype(BF16).astype(F32)
        middle = (decay - high).astype(BF16).astype(F32)
        low = decay - high - middle
        which = iota((16, 256), 0)
        out[at, 176:192, :] = jnp.where(
            which == 0, high, jnp.where(which == 1, middle, low)
        ).astype(BF16)

    def package(t):
        return pltpu.make_async_remote_copy(
            src_ref=pack.at[t], dst_ref=r_pack.at[chip], send_sem=send_a.at[t],
            recv_sem=recv_a.at[t], device_id=(me_d, target_chip(t) * 2 + core),
            device_id_type=MESH,
        )

    lax.fori_loop(0, AHEAD, compute, 0)
    pl.semaphore_wait(barrier, NS - 1 + ND - (home == me).astype(jnp.int32))
    lax.fori_loop(0, AHEAD, send_give, 0)

    def middle(t, _):
        combine(t - AHEAD, pack, t - AHEAD)
        compute(t, 0)
        package(t - AHEAD).start()
        send_give(t, 0)
        return 0

    lax.fori_loop(AHEAD, CHIPS, middle, 0)
    combine(CHIPS - AHEAD, pack, CHIPS - AHEAD)

    def rest(t, _):
        combine(t, pack, t)
        package(t - 1).start()
        return 0

    lax.fori_loop(CHIPS - AHEAD + 1, CHIPS - 1, rest, 0)
    combine(CHIPS - 1, r_pack, chip)
    package(CHIPS - 2).start()

    w_fetch.wait()
    narrow = w_own[...].astype(F32)
    same = (iota((256, 256), 0) // 64) == (iota((256, 256), 1) // 64)
    blocks_t = jnp.where(same, jnp.concatenate([narrow, narrow, narrow, narrow], axis=0), 0.0)
    blocks = jnp.transpose(blocks_t)
    weight = blocks.astype(BF16)
    skewed = (blocks_t - blocks).astype(BF16)
    carried[...] = jnp.zeros_like(carried)

    def wait_a(t, _):
        package(t).wait()
        return 0

    lax.fori_loop(0, CHIPS - 1, wait_a, 0)

    def chip_step(b, _):
        now = carried[...]
        queries = jnp.concatenate([r_pack[b, 128:160, 0:128], r_pack[b, 128:160, 128:256]], axis=0)
        past = dot(queries, now.astype(BF16))
        local = r_pack[b, 160:176, :].astype(F32)
        means[pl.ds(pl.multiple_of(b * 16, 16), 16), :] = local + jnp.concatenate(
            [by_head(past[:32]), by_head(past[32:])], axis=0
        )
        parts = r_pack[b, 176:192, :].astype(F32)
        decay = parts[0:1] + (parts[1:2] + parts[2:3])
        carried[...] = decay * now + r_pack[b, 0:128, :].astype(F32)
        return 0

    lax.fori_loop(0, CHIPS, chip_step, 0)

    def exchange(src, dst, send, recv, k):
        return pltpu.make_async_remote_copy(
            src_ref=src, dst_ref=dst, send_sem=send, recv_sem=recv,
            device_id=(me_d, peer(k)), device_id_type=MESH,
        )

    mean = means[...]
    square = dot(mean * mean, jnp.where(same, 1.0 / 64.0, 0.0), HI)
    pooled32 = mean / jnp.sqrt(square + EPS)
    pooled = pooled32.astype(BF16)
    projected = dot(pooled, weight).astype(BF16)
    margin_part[...] = dot_t(projected, pooled) - dot_t(pooled, projected)

    def margin_copy(k):
        rows = pl.ds(pl.multiple_of(peer(k) * 8, 8), 8)
        return exchange(margin_part.at[rows], r_margin.at[k], send_b.at[k], recv_b.at[k], k)

    def start_b(k, _):
        margin_copy(k).start()
        return 0

    lax.fori_loop(1, NS, start_b, 0)
    r_margin[0] = margin_part[pl.ds(pl.multiple_of(me * 8, 8), 8), :]
    skew_rows = dot(pooled, skewed).astype(BF16)
    pooled_t = jnp.transpose(pooled.astype(F32)).astype(BF16)
    ranks = jnp.broadcast_to(rank[...].astype(F32), (8, 128))
    mine = iota((8, 128), 1) == me * 8 + iota((8, 128), 0)
    own_rank = jnp.sum(jnp.where(mine, ranks, 0.0), axis=1, keepdims=True)
    target = jnp.where(own_rank < ranks, 1.0, jnp.where(own_rank > ranks, 0.0, 0.5))
    valid = mask[...].astype(F32)

    def wait_b(k, _):
        margin_copy(k).wait()
        return 0

    lax.fori_loop(1, NS, wait_b, 0)
    margin = jnp.sum(r_margin[...], axis=0)
    soft = jnp.maximum(margin, 0.0) + jnp.log(1.0 + jnp.exp(-jnp.abs(margin)))
    losses = jnp.sum(valid * (soft - target * margin), axis=0, keepdims=True)
    pair = 2.0 * valid * (1.0 / (1.0 + jnp.exp(-margin)) - target)
    loss_high = losses.astype(BF16).astype(F32)
    loss_rows = jnp.where(iota((8, 128), 0) == 0, loss_high, losses - loss_high)
    sent = jnp.concatenate([pair, loss_rows], axis=0).astype(BF16)
    pair_own[...] = sent
    r_pair[me] = sent

    def pair_copy(k):
        return exchange(pair_own, r_pair.at[me], send_c.at[k], recv_c.at[k], k)

    def start_c(k, _):
        pair_copy(k).start()
        return 0

    lax.fori_loop(1, NS, start_c, 0)

    def wait_c(k, _):
        pair_copy(k).wait()
        return 0

    lax.fori_loop(1, NS, wait_c, 0)
    pairs = r_pair[...].astype(F32)
    all_pair = pairs[:, :8, :].reshape(128, 128).astype(BF16)
    accumulated = dot(all_pair, pooled)
    high = accumulated.astype(BF16)
    low = (accumulated - high.astype(F32)).astype(BF16)
    product = (dot(pooled_t, high) + dot(pooled_t, low)) * (1.0 / 4096.0)
    for i in range(2 * NS):
        h = i // 8
        piece = product[i * 8 : i * 8 + 8, h * 64 : h * 64 + 64]
        w_part[i] = jnp.concatenate([piece[:4], piece[4:]], axis=1).astype(BF16)

    def w_copy(i):
        to_d = me * 2 + i // NS
        to_s = lax.rem(i, NS)
        return to_d, to_s, pltpu.make_async_remote_copy(
            src_ref=w_part.at[i],
            dst_ref=r_w.at[me_d],
            send_sem=send_w.at[i], recv_sem=recv_w.at[me_d],
            device_id=(to_d, to_s), device_id_type=MESH,
        )

    def start_w(i, _):
        to_d, to_s, c = w_copy(i)
        itself = jnp.logical_and(to_d == me_d, to_s == me)

        @pl.when(jnp.logical_not(itself))
        def _():
            c.start()

        @pl.when(itself)
        def _():
            r_w[me_d] = w_part[i]

        return 0

    lax.fori_loop(0, 2 * NS, start_w, 0)
    grad_part[...] = dot(all_pair, skew_rows).astype(BF16).reshape(NS, 8, 256)

    def grad_copy(k):
        return exchange(grad_part.at[peer(k)], r_grad.at[me], send_d.at[k], recv_d.at[k], k)

    def start_d(k, _):
        grad_copy(k).start()
        return 0

    lax.fori_loop(1, NS, start_d, 0)
    r_grad[me] = grad_part[me]
    loss_o[0] = jnp.sum(pairs[:, 8:10, :]) * (1.0 / (128.0 * 128.0))

    def wait_d(k, _):
        grad_copy(k).wait()
        return 0

    lax.fori_loop(1, NS, wait_d, 0)
    for b in range(NS):
        pg_o[:, b * 256 : b * 256 + 256] = r_grad[b].astype(F32)

    def wait_w(i, _):
        to_d, to_s, c = w_copy(i)

        @pl.when(jnp.logical_not(jnp.logical_and(to_d == me_d, to_s == me)))
        def _():
            c.wait_send()

        arrived = pltpu.make_async_remote_copy(
            src_ref=w_part.at[0], dst_ref=r_w.at[i],
            send_sem=send_w.at[i], recv_sem=recv_w.at[i],
            device_id=(to_d, to_s), device_id_type=MESH,
        )

        @pl.when(jnp.logical_or(i != me_d, home != me))
        def _():
            arrived.wait_recv()

        return 0

    lax.fori_loop(0, ND, wait_w, 0)
    folded = jnp.sum(r_w[...].astype(F32), axis=0)
    wg_o[...] = jnp.concatenate([folded[:, :64], folded[:, 64:]], axis=0)


def per_device(
    token_input, input_map, output_map, step_size, forget, skip_gain, segments, yield_rank,
    pair_mask, comparator,
):
    vmem = pl.BlockSpec(memory_space=pltpu.VMEM)
    smem = pl.BlockSpec(memory_space=pltpu.SMEM)
    shape = jax.ShapeDtypeStruct
    sem = pltpu.SemaphoreType.DMA
    pooled_grad, loss, weight_grad = pl.pallas_call(
        list_kernel,
        out_shape=(shape((8, 4096), F32), shape((1,), F32), shape((8, 64), F32)),
        in_specs=[smem] + [vmem] * 6 + [pl.BlockSpec(memory_space=pl.ANY)] + [vmem] * 2,
        out_specs=(vmem, smem, vmem),
        scratch_shapes=[
            pltpu.VMEM((128, 128), F32),
            pltpu.VMEM((64, 128), F32),
            pltpu.VMEM((8, 160, 256), BF16),
            pltpu.VMEM((8, 16, 256), F32),
            pltpu.VMEM((8, 160, 256), BF16),
            pltpu.VMEM((8, 16, 256), F32),
            pltpu.VMEM((8, 160, 256), BF16),
            pltpu.VMEM((8, 16, 256), F32),
            pltpu.VMEM((7, 192, 256), BF16),
            pltpu.VMEM((8, 192, 256), BF16),
            pltpu.VMEM((64, 256), BF16),
            pltpu.VMEM((128, 256), F32),
            pltpu.VMEM((128, 256), F32),
            pltpu.VMEM((128, 128), F32),
            pltpu.VMEM((16, 8, 128), F32),
            pltpu.VMEM((16, 128), BF16),
            pltpu.VMEM((16, 16, 128), BF16),
            pltpu.VMEM((16, 8, 256), BF16),
            pltpu.VMEM((16, 8, 256), BF16),
            pltpu.VMEM((32, 4, 128), BF16),
            pltpu.VMEM((32, 4, 128), BF16),
            sem((8,)), sem((8,)), sem((8,)), sem((8,)), sem((7,)), sem((7,)),
            sem((16,)), sem((16,)), sem((16,)), sem((16,)), sem((16,)), sem((16,)),
            sem((32,)), sem((32,)), sem(()),
        ],
        compiler_params=pltpu.CompilerParams(collective_id=0, has_side_effects=True),
        name="list",
    )(
        skip_gain, token_input[0], input_map[0], output_map[0], step_size[0].T, forget[0].T,
        segments[0], comparator.T, yield_rank, pair_mask[0],
    )
    return (loss, pooled_grad[None], weight_grad)


def solution(mesh):
    return jax.shard_map(
        per_device,
        mesh=mesh,
        in_specs=(
            P("dp", "seq", None),
            P("dp", "seq", None),
            P("dp", "seq", None),
            P("dp", "seq", None),
            P("dp", "seq", None),
            P(),
            P("dp", "seq", None),
            P("dp", None),
            P("dp", "seq", None),
            P(),
        ),
        out_specs=(P("dp"), P("dp", "seq", None), P(("dp", "seq"), None)),
        check_vma=False,
    )
```

time: 103 us -> 66.8 us (0.65)
  Pallas kernels: 95.3 us -> 62 us
  local copies, waits for them, and re-layouts: 6.62 us -> 2.17 us
  between operations: 0.66 us -> 2.41 us
    pallas_call x2 -> x1, Pallas kernels: 95.3 us -> 62 us  [per_device(): pl.pallas_call(list_kernel, out_shape=(shape((8, 4096), F32), shape((1,),...]
    unnamed x13 -> x4, local copies, waits for them, and re-layouts: 5.43 us -> 2.17 us
    slice x1 -> x0, local copies, waits for them, and re-layouts: 1.19 us -> none  [per_device(): return (loss[0, :1], pooled_grad[None], weight_grad)]
where the time goes in v2:
time: 66.8 us; the launch traced here: 66.6 us
  Pallas kernels  62 us (93%)
  between operations  2.41 us (4%)
  local copies, waits for them, and re-layouts  2.17 us (3%)
    pallas_call x1, Pallas kernels, per_device(): pl.pallas_call(list_kernel, out_shape=(shape((8, 4096), F32), shape((1,),...  62 us
    unnamed x4, local copies, waits for them, and re-layouts  2.17 us

profile of v2, /device:TPU:1, one launch (start us, length us, event | category | flops | bytes accessed | tf_op | source)
XLA Modules:
  0.0 66.6 jit_solution(14182622947344246319)
XLA Ops:
  0.6 62.0 %list.1 = (f32[8,4096]{1,0:T(8,128)}, f32[1]{0:T(128)}, f32[8,64]{1,0:T(8,128)}) custom-call(f32[64]{0:T(128)} %skip.1, bf16[128,4096]{1,0:T(8,128)(2,1)} %bitcast.13, bf16[128,128]{1,0:T(8,128)(2,1)} %bitcast.16, bf16[128,128]{1,0:T(8,128)(2,1)} %bitcast.17, f32[64,128]{1,0:T(8,128)} %bitcast.18, f32[64,128]{1,0:T(8,128)} %bitcast.19, s32[1,128]{1,0:T(1,128)} %bitcast.21, ...), custom_call_target="tpu_custom_call" | custom-call | tf_op jit(solution)/shard_map/list/pallas_call | solution.py:394
  63.3 0.0 copy-start
  63.3 1.6 %copy.17 = f32[1,8,4096]{2,1,0:T(8,128)} copy(f32[1,8,4096]{2,1,0:T(8,128)} %bitcast.15) | data formatting | bytes 262144
  64.9 0.0 copy-done
  64.9 0.6 copy.18
Async XLA Ops:
  63.3 1.6 %copy-start = (f32[8,64]{1,0:T(8,128)S(1)}, f32[8,64]{1,0:T(8,128)}, u32[]{:S(2)}) copy-start(f32[8,64]{1,0:T(8,128)} %get-tuple-element.14) | copy-start | bytes 6148

commit v3 on v2

--- a/solution.py
+++ b/solution.py
@@ -12,7 +12,7 @@
 NS = 16
 ND = 32
 CHIPS = 8
-AHEAD = 4
+AHEAD = 2
 MESH = pl.DeviceIdType.MESH
 
 
@@ -33,9 +33,10 @@
 def list_kernel(
     skip, tok, b_in, c_out, step, forget, seg, w_in, rank, mask,
     pg_o, loss_o, wg_o,
-    cols, dl_rows, give_s, give_m, own_s, own_m, got_s, got_m, pack, r_pack, w_own,
+    cols, dl_rows, give_s, give_m, own_s, own_m, got_s, got_m, pack, pack_d,
+    r_pack, r_dec, relay, relay_d, w_own,
     carried, means, margin_part, r_margin, pair_own, r_pair, grad_part, r_grad, w_part, r_w,
-    send_g, recv_g, send_m, recv_m, send_a, recv_a, send_b, recv_b, send_c, recv_c,
+    send_g, recv_g, send_m, recv_m, send_a, recv_a, send_ad, recv_ad, hop_s, hop_r, send_b, recv_b, send_c, recv_c,
     send_d, recv_d, send_w, recv_w, w_sem,
 ):
     me_d = lax.axis_index("dp")
@@ -148,7 +149,7 @@
             total = total + jnp.where(lane == h, rows[h * 8 : h * 8 + 8], 0.0)
         return total
 
-    def combine(t, out, at):
+    def combine(t, out, out_d, at):
         for c in give(t):
             c.wait()
         first = core == 0
@@ -174,43 +175,88 @@
             [early_m[0:8], late_m[0:8] + within], axis=0
         ).astype(BF16)
         decay = early_d * late_d
-        high = decay.astype(BF16).astype(F32)
-        middle = (decay - high).astype(BF16).astype(F32)
-        low = decay - high - middle
-        which = iota((16, 256), 0)
-        out[at, 176:192, :] = jnp.where(
-            which == 0, high, jnp.where(which == 1, middle, low)
-        ).astype(BF16)
+        out_d[at] = jnp.concatenate([decay[:, :128], decay[:, 128:]], axis=0)
 
     def package(t):
-        return pltpu.make_async_remote_copy(
-            src_ref=pack.at[t], dst_ref=r_pack.at[chip], send_sem=send_a.at[t],
-            recv_sem=recv_a.at[t], device_id=(me_d, target_chip(t) * 2 + core),
-            device_id_type=MESH,
-        )
+        to = (me_d, target_chip(t) * 2 + core)
+        return (
+            pltpu.make_async_remote_copy(
+                src_ref=pack.at[t], dst_ref=r_pack.at[chip], send_sem=send_a.at[t],
+                recv_sem=recv_a.at[t], device_id=to, device_id_type=MESH,
+            ),
+            pltpu.make_async_remote_copy(
+                src_ref=pack_d.at[t], dst_ref=r_dec.at[chip], send_sem=send_ad.at[t],
+                recv_sem=recv_ad.at[t], device_id=to, device_id_type=MESH,
+            ),
+        )
+
+    way = 1 - 2 * core
+
+    def chip_at(away):
+        return lax.rem(chip + away * way + CHIPS, CHIPS)
+
+    hop_to = (me_d, chip_at(1) * 2 + core)
+    to_relay = (
+        pltpu.make_async_remote_copy(
+            src_ref=pack.at[0], dst_ref=relay, send_sem=hop_s.at[0], recv_sem=hop_r.at[0],
+            device_id=hop_to, device_id_type=MESH,
+        ),
+        pltpu.make_async_remote_copy(
+            src_ref=pack_d.at[0], dst_ref=relay_d, send_sem=hop_s.at[1], recv_sem=hop_r.at[1],
+            device_id=hop_to, device_id_type=MESH,
+        ),
+    )
+    end_at = (me_d, chip_at(3) * 2 + core)
+    origin = chip_at(-1)
+    forward = (
+        pltpu.make_async_remote_copy(
+            src_ref=relay, dst_ref=r_pack.at[origin], send_sem=send_a.at[0],
+            recv_sem=recv_a.at[0], device_id=end_at, device_id_type=MESH,
+        ),
+        pltpu.make_async_remote_copy(
+            src_ref=relay_d, dst_ref=r_dec.at[origin], send_sem=send_ad.at[0],
+            recv_sem=recv_ad.at[0], device_id=end_at, device_id_type=MESH,
+        ),
+    )
+
+    def send_package(t):
+        @pl.when(t == 0)
+        def _():
+            for c in to_relay:
+                c.start()
+
+        @pl.when(t > 0)
+        def _():
+            for c in package(t):
+                c.start()
 
     lax.fori_loop(0, AHEAD, compute, 0)
     pl.semaphore_wait(barrier, NS - 1 + ND - (home == me).astype(jnp.int32))
     lax.fori_loop(0, AHEAD, send_give, 0)
 
     def middle(t, _):
-        combine(t - AHEAD, pack, t - AHEAD)
+        combine(t - AHEAD, pack, pack_d, t - AHEAD)
         compute(t, 0)
-        package(t - AHEAD).start()
+        send_package(t - AHEAD)
         send_give(t, 0)
         return 0
 
     lax.fori_loop(AHEAD, CHIPS, middle, 0)
-    combine(CHIPS - AHEAD, pack, CHIPS - AHEAD)
+    combine(CHIPS - AHEAD, pack, pack_d, CHIPS - AHEAD)
+    for c in to_relay:
+        c.wait_recv()
+    for c in forward:
+        c.start()
 
     def rest(t, _):
-        combine(t, pack, t)
-        package(t - 1).start()
+        combine(t, pack, pack_d, t)
+        send_package(t - 1)
         return 0
 
     lax.fori_loop(CHIPS - AHEAD + 1, CHIPS - 1, rest, 0)
-    combine(CHIPS - 1, r_pack, chip)
-    package(CHIPS - 2).start()
+    combine(CHIPS - 1, r_pack, r_dec, chip)
+    for c in package(CHIPS - 2):
+        c.start()
 
     w_fetch.wait()
     narrow = w_own[...].astype(F32)
@@ -221,13 +267,16 @@
     skewed = (blocks_t - blocks).astype(BF16)
     carried[...] = jnp.zeros_like(carried)
 
-    def wait_a(t, _):
-        package(t).wait()
-        return 0
-
-    lax.fori_loop(0, CHIPS - 1, wait_a, 0)
-
     def chip_step(b, _):
+        away = lax.rem(chip - b + CHIPS, CHIPS)
+        half = CHIPS // 2
+        order = jnp.where(away < half, CHIPS - 1 - 2 * away, 2 * (away - half))
+
+        @pl.when(b != chip)
+        def _():
+            for c in package(order):
+                c.wait_recv()
+
         now = carried[...]
         queries = jnp.concatenate([r_pack[b, 128:160, 0:128], r_pack[b, 128:160, 128:256]], axis=0)
         past = dot(queries, now.astype(BF16))
@@ -235,8 +284,7 @@
         means[pl.ds(pl.multiple_of(b * 16, 16), 16), :] = local + jnp.concatenate(
             [by_head(past[:32]), by_head(past[32:])], axis=0
         )
-        parts = r_pack[b, 176:192, :].astype(F32)
-        decay = parts[0:1] + (parts[1:2] + parts[2:3])
+        decay = jnp.concatenate([r_dec[b, 0:1, :], r_dec[b, 1:2, :]], axis=1)
         carried[...] = decay * now + r_pack[b, 0:128, :].astype(F32)
         return 0
 
@@ -351,13 +399,23 @@
     r_grad[me] = grad_part[me]
     loss_o[0] = jnp.sum(pairs[:, 8:10, :]) * (1.0 / (128.0 * 128.0))
 
+    for c in to_relay:
+        c.wait_send()
+
+    def wait_a(t, _):
+        for c in package(t):
+            c.wait_send()
+        return 0
+
+    lax.fori_loop(0, CHIPS - 1, wait_a, 0)
+
     def wait_d(k, _):
         grad_copy(k).wait()
         return 0
 
     lax.fori_loop(1, NS, wait_d, 0)
     for b in range(NS):
-        pg_o[:, b * 256 : b * 256 + 256] = r_grad[b].astype(F32)
+        pg_o[:, b * 256 : b * 256 + 256] = r_grad[b]
 
     def wait_w(i, _):
         to_d, to_s, c = w_copy(i)
@@ -393,7 +451,7 @@
     sem = pltpu.SemaphoreType.DMA
     pooled_grad, loss, weight_grad = pl.pallas_call(
         list_kernel,
-        out_shape=(shape((8, 4096), F32), shape((1,), F32), shape((8, 64), F32)),
+        out_shape=(shape((8, 4096), BF16), shape((1,), F32), shape((8, 64), F32)),
         in_specs=[smem] + [vmem] * 6 + [pl.BlockSpec(memory_space=pl.ANY)] + [vmem] * 2,
         out_specs=(vmem, smem, vmem),
         scratch_shapes=[
@@ -405,8 +463,12 @@
             pltpu.VMEM((8, 16, 256), F32),
             pltpu.VMEM((8, 160, 256), BF16),
             pltpu.VMEM((8, 16, 256), F32),
-            pltpu.VMEM((7, 192, 256), BF16),
-            pltpu.VMEM((8, 192, 256), BF16),
+            pltpu.VMEM((7, 176, 256), BF16),
+            pltpu.VMEM((7, 2, 128), F32),
+            pltpu.VMEM((8, 176, 256), BF16),
+            pltpu.VMEM((8, 2, 128), F32),
+            pltpu.VMEM((176, 256), BF16),
+            pltpu.VMEM((2, 128), F32),
             pltpu.VMEM((64, 256), BF16),
             pltpu.VMEM((128, 256), F32),
             pltpu.VMEM((128, 256), F32),
@@ -419,6 +481,7 @@
             pltpu.VMEM((32, 4, 128), BF16),
             pltpu.VMEM((32, 4, 128), BF16),
             sem((8,)), sem((8,)), sem((8,)), sem((8,)), sem((7,)), sem((7,)),
+            sem((7,)), sem((7,)), sem((2,)), sem((2,)),
             sem((16,)), sem((16,)), sem((16,)), sem((16,)), sem((16,)), sem((16,)),
             sem((32,)), sem((32,)), sem(()),
         ],
@@ -428,7 +491,7 @@
         skip_gain, token_input[0], input_map[0], output_map[0], step_size[0].T, forget[0].T,
         segments[0], comparator.T, yield_rank, pair_mask[0],
     )
-    return (loss, pooled_grad[None], weight_grad)
+    return (loss, pooled_grad.astype(F32)[None], weight_grad)
 
 
 def solution(mesh):

time: 66.8 us -> 65.9 us (0.987)
  local copies, waits for them, and re-layouts: 2.17 us -> 0.6 us
  other arithmetic: 0 us -> 1.5 us
  Pallas kernels: 62 us -> 61.1 us
    unnamed x4 -> x3, local copies, waits for them, and re-layouts: 2.17 us -> 0.6 us
    broadcast_in_dim x0 -> x1, other arithmetic: none -> 1.5 us  [per_device(): return (loss, pooled_grad.astype(F32)[None], weight_grad)]
    pallas_call x1, Pallas kernels: 62 us -> 61.1 us  [per_device(): pl.pallas_call(list_kernel, out_shape=(shape((8, 4096), BF16), shape((1,)...]
where the time goes in v3:
time: 65.9 us; the launch traced here: 65.7 us
  Pallas kernels  61.1 us (93%)
  between operations  2.48 us (4%)
  other arithmetic  1.5 us (2%)
    pallas_call x1, Pallas kernels, per_device(): pl.pallas_call(list_kernel, out_shape=(shape((8, 4096), BF16), shape((1,)...  61.1 us
    broadcast_in_dim x1, other arithmetic, per_device(): return (loss, pooled_grad.astype(F32)[None], weight_grad)  1.5 us

profile of v3, /device:TPU:1, one launch (start us, length us, event | category | flops | bytes accessed | tf_op | source)
XLA Modules:
  0.0 65.7 jit_solution(15052174555819884992)
XLA Ops:
  0.6 61.1 %list.1 = (bf16[8,4096]{1,0:T(8,128)(2,1)}, f32[1]{0:T(128)}, f32[8,64]{1,0:T(8,128)}) custom-call(f32[64]{0:T(128)} %skip.1, bf16[128,4096]{1,0:T(8,128)(2,1)} %bitcast.15, bf16[128,128]{1,0:T(8,128)(2,1)} %bitcast.17, bf16[128,128]{1,0:T(8,128)(2,1)} %bitcast.18, f32[64,128]{1,0:T(8,128)} %bitcast.19, f32[64,128]{1,0:T(8,128)} %bitcast.20, ...), custom_call_target="tpu_custom_call" | custom-call | tf_op jit(solution)/shard_map/list/pallas_call | solution.py:452
  61.8 0.0 copy-start
  61.8 1.5 %bitcast_convert_fusion = f32[1,8,4096]{2,1,0:T(8,128)} fusion(bf16[8,4096]{1,0:T(8,128)(2,1)} %get-tuple-element.7), kind=kLoop, calls=%fused_computation | loop fusion | flops 32768 | bytes 196608 | tf_op jit(solution)/shard_map/broadcast_in_dim | solution.py:494
  64.0 0.0 copy-done
  64.0 0.6 copy.16
Async XLA Ops:
  61.8 2.2 %copy-start = (f32[8,64]{1,0:T(8,128)S(1)}, f32[8,64]{1,0:T(8,128)}, u32[]{:S(2)}) copy-start(f32[8,64]{1,0:T(8,128)} %get-tuple-element.14) | copy-start | bytes 6148

commit v4 on v3

--- a/solution.py
+++ b/solution.py
@@ -11,6 +11,7 @@
 EPS = 1e-05
 NS = 16
 ND = 32
+COLS = 4
 CHIPS = 8
 AHEAD = 2
 MESH = pl.DeviceIdType.MESH
@@ -37,7 +38,7 @@
     r_pack, r_dec, relay, relay_d, w_own,
     carried, means, margin_part, r_margin, pair_own, r_pair, grad_part, r_grad, w_part, r_w,
     send_g, recv_g, send_m, recv_m, send_a, recv_a, send_ad, recv_ad, hop_s, hop_r, send_b, recv_b, send_c, recv_c,
-    send_d, recv_d, send_w, recv_w, w_sem,
+    send_d, recv_d, send_w, recv_w, w_sem, line_sem, plane_sem,
 ):
     me_d = lax.axis_index("dp")
     me = lax.axis_index("seq")
@@ -50,20 +51,19 @@
 
     barrier = pltpu.get_barrier_semaphore()
 
-    def greet_source(s, _):
-        @pl.when(jnp.logical_or(s != me_d, home != me))
-        def _():
-            pl.semaphore_signal(barrier, inc=1, device_id=(s, home), device_id_type=MESH)
-
-        return 0
-
-    lax.fori_loop(0, ND, greet_source, 0)
-
     def greet(k, _):
         pl.semaphore_signal(barrier, inc=1, device_id=(me_d, peer(k)), device_id_type=MESH)
         return 0
 
     lax.fori_loop(1, NS, greet, 0)
+    rows_y, cols_x = ND // COLS, COLS
+    at_y, at_x = me_d // COLS, lax.rem(me_d, COLS)
+    for k in range(1, rows_y):
+        there = lax.rem(at_y + k, rows_y) * COLS + at_x
+        pl.semaphore_signal(barrier, inc=1, device_id=(there, me), device_id_type=MESH)
+    beside = [(at_y * COLS + lax.rem(at_x + k, cols_x), me) for k in range(1, cols_x)]
+    for there in beside:
+        pl.semaphore_signal(barrier, inc=1, device_id=there, device_id_type=MESH)
     w_fetch = pltpu.make_async_copy(
         w_in.at[:, pl.ds(pl.multiple_of(me * 256, 256), 256)], w_own, w_sem
     )
@@ -231,7 +231,9 @@
                 c.start()
 
     lax.fori_loop(0, AHEAD, compute, 0)
-    pl.semaphore_wait(barrier, NS - 1 + ND - (home == me).astype(jnp.int32))
+    pl.semaphore_wait(barrier, NS - 1 + rows_y - 1 + cols_x - 1)
+    for there in beside:
+        pl.semaphore_signal(line_sem, inc=1, device_id=there, device_id_type=MESH)
     lax.fori_loop(0, AHEAD, send_give, 0)
 
     def middle(t, _):
@@ -258,6 +260,13 @@
     for c in package(CHIPS - 2):
         c.start()
 
+    pl.semaphore_wait(line_sem, cols_x - 1)
+
+    def tell(k, _):
+        pl.semaphore_signal(plane_sem, inc=1, device_id=(me_d, peer(k)), device_id_type=MESH)
+        return 0
+
+    lax.fori_loop(1, NS, tell, 0)
     w_fetch.wait()
     narrow = w_own[...].astype(F32)
     same = (iota((256, 256), 0) // 64) == (iota((256, 256), 1) // 64)
@@ -265,6 +274,7 @@
     blocks = jnp.transpose(blocks_t)
     weight = blocks.astype(BF16)
     skewed = (blocks_t - blocks).astype(BF16)
+    spread = jnp.where(same, 1.0 / 64.0, 0.0).astype(BF16)
     carried[...] = jnp.zeros_like(carried)
 
     def chip_step(b, _):
@@ -297,9 +307,11 @@
         )
 
     mean = means[...]
-    square = dot(mean * mean, jnp.where(same, 1.0 / 64.0, 0.0), HI)
-    pooled32 = mean / jnp.sqrt(square + EPS)
-    pooled = pooled32.astype(BF16)
+    squared = mean * mean
+    squared_high = squared.astype(BF16)
+    squared_low = (squared - squared_high.astype(F32)).astype(BF16)
+    square = dot(squared_high, spread) + dot(squared_low, spread)
+    pooled = (mean * lax.rsqrt(square + EPS)).astype(BF16)
     projected = dot(pooled, weight).astype(BF16)
     margin_part[...] = dot_t(projected, pooled) - dot_t(pooled, projected)
 
@@ -311,7 +323,7 @@
         margin_copy(k).start()
         return 0
 
-    lax.fori_loop(1, NS, start_b, 0)
+    lax.fori_loop(1, NS, start_b, 0, unroll=True)
     r_margin[0] = margin_part[pl.ds(pl.multiple_of(me * 8, 8), 8), :]
     skew_rows = dot(pooled, skewed).astype(BF16)
     pooled_t = jnp.transpose(pooled.astype(F32)).astype(BF16)
@@ -343,7 +355,9 @@
         pair_copy(k).start()
         return 0
 
-    lax.fori_loop(1, NS, start_c, 0)
+    lax.fori_loop(1, NS, start_c, 0, unroll=True)
+
+    pl.semaphore_wait(plane_sem, NS - 1)
 
     def wait_c(k, _):
         pair_copy(k).wait()
@@ -385,7 +399,7 @@
 
         return 0
 
-    lax.fori_loop(0, 2 * NS, start_w, 0)
+    lax.fori_loop(0, 2 * NS, start_w, 0, unroll=4)
     grad_part[...] = dot(all_pair, skew_rows).astype(BF16).reshape(NS, 8, 256)
 
     def grad_copy(k):
@@ -395,7 +409,7 @@
         grad_copy(k).start()
         return 0
 
-    lax.fori_loop(1, NS, start_d, 0)
+    lax.fori_loop(1, NS, start_d, 0, unroll=True)
     r_grad[me] = grad_part[me]
     loss_o[0] = jnp.sum(pairs[:, 8:10, :]) * (1.0 / (128.0 * 128.0))
 
@@ -484,6 +498,7 @@
             sem((7,)), sem((7,)), sem((2,)), sem((2,)),
             sem((16,)), sem((16,)), sem((16,)), sem((16,)), sem((16,)), sem((16,)),
             sem((32,)), sem((32,)), sem(()),
+            pltpu.SemaphoreType.REGULAR, pltpu.SemaphoreType.REGULAR,
         ],
         compiler_params=pltpu.CompilerParams(collective_id=0, has_side_effects=True),
         name="list",

time: 65.9 us -> 63 us (0.956)
  Pallas kernels: 61.1 us -> 58.2 us
    pallas_call x1, Pallas kernels: 61.1 us -> 58.2 us  [per_device(): pl.pallas_call(list_kernel, out_shape=(shape((8, 4096), BF16), shape((1,)...]
where the time goes in v4:
time: 63 us; the launch traced here: 62.8 us
  Pallas kernels  58.2 us (92%)
  between operations  2.48 us (4%)
  other arithmetic  1.5 us (2%)
    pallas_call x1, Pallas kernels, per_device(): pl.pallas_call(list_kernel, out_shape=(shape((8, 4096), BF16), shape((1,)...  58.2 us
    broadcast_in_dim x1, other arithmetic, per_device(): return (loss, pooled_grad.astype(F32)[None], weight_grad)  1.5 us

profile of v4, /device:TPU:1, one launch (start us, length us, event | category | flops | bytes accessed | tf_op | source)
XLA Modules:
  0.0 62.8 jit_solution(10587981685789333636)
XLA Ops:
  0.6 58.2 %list.1 = (bf16[8,4096]{1,0:T(8,128)(2,1)}, f32[1]{0:T(128)}, f32[8,64]{1,0:T(8,128)}) custom-call(f32[64]{0:T(128)} %skip.1, bf16[128,4096]{1,0:T(8,128)(2,1)} %bitcast.15, bf16[128,128]{1,0:T(8,128)(2,1)} %bitcast.17, bf16[128,128]{1,0:T(8,128)(2,1)} %bitcast.18, f32[64,128]{1,0:T(8,128)} %bitcast.19, f32[64,128]{1,0:T(8,128)} %bitcast.20, ...), custom_call_target="tpu_custom_call" | custom-call | tf_op jit(solution)/shard_map/list/pallas_call | solution.py:466
  58.9 0.0 copy-start
  58.9 1.5 %bitcast_convert_fusion = f32[1,8,4096]{2,1,0:T(8,128)} fusion(bf16[8,4096]{1,0:T(8,128)(2,1)} %get-tuple-element.7), kind=kLoop, calls=%fused_computation | loop fusion | flops 32768 | bytes 196608 | tf_op jit(solution)/shard_map/broadcast_in_dim | solution.py:509
  61.1 0.0 copy-done
  61.1 0.6 copy.16
Async XLA Ops:
  58.9 2.2 %copy-start = (f32[8,64]{1,0:T(8,128)S(1)}, f32[8,64]{1,0:T(8,128)}, u32[]{:S(2)}) copy-start(f32[8,64]{1,0:T(8,128)} %get-tuple-element.14) | copy-start | bytes 6148

commit v5 on v4

--- a/solution.py
+++ b/solution.py
@@ -34,10 +34,11 @@
 def list_kernel(
     skip, tok, b_in, c_out, step, forget, seg, w_in, rank, mask,
     pg_o, loss_o, wg_o,
-    cols, dl_rows, give_s, give_m, own_s, own_m, got_s, got_m, pack, pack_d,
+    cols, dl_rows, give_s, give_q, give_m, give_d, own_s, own_q, own_m, own_d,
+    got_s, got_q, got_m, got_d, pack, pack_d,
     r_pack, r_dec, relay, relay_d, w_own,
     carried, means, margin_part, r_margin, pair_own, r_pair, grad_part, r_grad, w_part, r_w,
-    send_g, recv_g, send_m, recv_m, send_a, recv_a, send_ad, recv_ad, hop_s, hop_r, send_b, recv_b, send_c, recv_c,
+    send_g, recv_g, send_a, recv_a, send_ad, recv_ad, hop_s, hop_r, send_b, recv_b, send_c, recv_c,
     send_d, recv_d, send_w, recv_w, w_sem, line_sem, plane_sem,
 ):
     me_d = lax.axis_index("dp")
@@ -84,7 +85,12 @@
     left = iota((128, 128), 1) < 64
     left8 = left[:8]
 
-    def group(j, out_s, out_m, t):
+    gives = (give_s, give_q, give_m, give_d)
+    owns = (own_s, own_q, own_m, own_d)
+    gots = (got_s, got_q, got_m, got_d)
+
+    def group(j, outs, t):
+        out_s, out_q, out_m, out_d = outs
         here = pltpu.roll(cols[...], lax.rem(128 - 4 * j, 128), 1)
         query_rows = []
         for pair in range(2):
@@ -103,15 +109,14 @@
                 query_rows.append(average * past)
                 totals.append(past[:, 127:128])
             both = dot(jnp.concatenate(mixed, axis=0).astype(BF16), tokens)
-            out_m[t, 0:8, at_lanes] = jnp.where(left8, both[:8], both[8:]) * inverse
-            out_m[t, 8:16, at_lanes] = jnp.where(left8, totals[0], totals[1])
+            out_m[t, :, at_lanes] = jnp.where(left8, both[:8], both[8:]) * inverse
+            out_d[t, pair : pair + 1, :] = jnp.where(left8[:1], totals[0], totals[1])
             base = 64 + pair * 2
             weight = jnp.where(left, here[:, base : base + 1], here[:, base + 1 : base + 2])
             scaled = (tokens.astype(F32) * weight).astype(BF16)
-            out_s[t, 0:128, at_lanes] = dot(b_t, scaled).astype(BF16)
-        queries = dot(jnp.concatenate(query_rows, axis=0).astype(BF16), c_out[...]).astype(BF16)
-        out_s[t, 128:160, 0:128] = queries
-        out_s[t, 128:160, 128:256] = queries
+            out_s[t, :, at_lanes] = dot(b_t, scaled).astype(BF16)
+        queries = dot(jnp.concatenate(query_rows, axis=0).astype(BF16), c_out[...])
+        out_q[t] = queries.astype(BF16)
 
     def target_chip(t):
         away = CHIPS // 2 + (t // 2 + lax.rem(t, 2)) * (1 - 2 * lax.rem(t, 2))
@@ -119,22 +124,19 @@
 
     def compute(t, _):
         to = target_chip(t) * 2
-        group(to + 1 - core, give_s, give_m, t)
-        group(to + core, own_s, own_m, t)
+        group(to + 1 - core, gives, t)
+        group(to + core, owns, t)
         return 0
 
     def give(t):
         other = (me_d, chip * 2 + 1 - core)
-        return (
+        return [
             pltpu.make_async_remote_copy(
-                src_ref=give_s.at[t], dst_ref=got_s.at[t], send_sem=send_g.at[t],
-                recv_sem=recv_g.at[t], device_id=other, device_id_type=MESH,
-            ),
-            pltpu.make_async_remote_copy(
-                src_ref=give_m.at[t], dst_ref=got_m.at[t], send_sem=send_m.at[t],
-                recv_sem=recv_m.at[t], device_id=other, device_id_type=MESH,
-            ),
-        )
+                src_ref=src.at[t], dst_ref=dst.at[t], send_sem=send_g.at[n, t],
+                recv_sem=recv_g.at[n, t], device_id=other, device_id_type=MESH,
+            )
+            for n, (src, dst) in enumerate(zip(gives, gots))
+        ]
 
     def send_give(t, _):
         for c in give(t):
@@ -153,29 +155,31 @@
         for c in give(t):
             c.wait()
         first = core == 0
-        mine, theirs = own_s[t], got_s[t]
-        early = jnp.where(first, mine, theirs)
-        late = jnp.where(first, theirs, mine)
-        mine_m, theirs_m = own_m[t], got_m[t]
-        early_m = jnp.where(first, mine_m, theirs_m)
-        late_m = jnp.where(first, theirs_m, mine_m)
-        early_d, late_d = early_m[8:9, :], late_m[8:9, :]
-        state = late_d * early[:128].astype(F32) + late[:128].astype(F32)
-        late_q = late[128:160, 0:128]
-        within = by_head(dot(late_q, early[:128]))
+
+        def ordered(n):
+            mine, theirs = owns[n][t], gots[n][t]
+            return jnp.where(first, mine, theirs), jnp.where(first, theirs, mine)
+
+        early, late = ordered(0)
+        early_q, late_q = ordered(1)
+        early_m, late_m = ordered(2)
+        early_2, late_2 = ordered(3)
+        early_d = jnp.concatenate([early_2[0:1], early_2[1:2]], axis=1)
+        late_d = jnp.concatenate([late_2[0:1], late_2[1:2]], axis=1)
+        state = late_d * early.astype(F32) + late.astype(F32)
+        within = by_head(dot(late_q, early))
         scaled_q = late_q.astype(F32)
         scaled_q = jnp.concatenate(
             [scaled_q[h * 8 : h * 8 + 8] * early_d[:, h * 64 : h * 64 + 1] for h in range(4)],
             axis=0,
         )
         out[at, 0:128, :] = state.astype(BF16)
-        out[at, 128:160, 0:128] = early[128:160, 0:128]
+        out[at, 128:160, 0:128] = early_q
         out[at, 128:160, 128:256] = scaled_q.astype(BF16)
         out[at, 160:176, :] = jnp.concatenate(
-            [early_m[0:8], late_m[0:8] + within], axis=0
+            [early_m, late_m + within], axis=0
         ).astype(BF16)
-        decay = early_d * late_d
-        out_d[at] = jnp.concatenate([decay[:, :128], decay[:, 128:]], axis=0)
+        out_d[at] = early_2 * late_2
 
     def package(t):
         to = (me_d, target_chip(t) * 2 + core)
@@ -471,12 +475,18 @@
         scratch_shapes=[
             pltpu.VMEM((128, 128), F32),
             pltpu.VMEM((64, 128), F32),
-            pltpu.VMEM((8, 160, 256), BF16),
-            pltpu.VMEM((8, 16, 256), F32),
-            pltpu.VMEM((8, 160, 256), BF16),
-            pltpu.VMEM((8, 16, 256), F32),
-            pltpu.VMEM((8, 160, 256), BF16),
-            pltpu.VMEM((8, 16, 256), F32),
+            pltpu.VMEM((8, 128, 256), BF16),
+            pltpu.VMEM((8, 32, 128), BF16),
+            pltpu.VMEM((8, 8, 256), F32),
+            pltpu.VMEM((8, 2, 128), F32),
+            pltpu.VMEM((8, 128, 256), BF16),
+            pltpu.VMEM((8, 32, 128), BF16),
+            pltpu.VMEM((8, 8, 256), F32),
+            pltpu.VMEM((8, 2, 128), F32),
+            pltpu.VMEM((8, 128, 256), BF16),
+            pltpu.VMEM((8, 32, 128), BF16),
+            pltpu.VMEM((8, 8, 256), F32),
+            pltpu.VMEM((8, 2, 128), F32),
             pltpu.VMEM((7, 176, 256), BF16),
             pltpu.VMEM((7, 2, 128), F32),
             pltpu.VMEM((8, 176, 256), BF16),
@@ -494,7 +504,7 @@
             pltpu.VMEM((16, 8, 256), BF16),
             pltpu.VMEM((32, 4, 128), BF16),
             pltpu.VMEM((32, 4, 128), BF16),
-            sem((8,)), sem((8,)), sem((8,)), sem((8,)), sem((7,)), sem((7,)),
+            sem((4, 8)), sem((4, 8)), sem((7,)), sem((7,)),
             sem((7,)), sem((7,)), sem((2,)), sem((2,)),
             sem((16,)), sem((16,)), sem((16,)), sem((16,)), sem((16,)), sem((16,)),
             sem((32,)), sem((32,)), sem(()),

time: 63 us -> 63.3 us (level)
  no operation moved by 1% of the time
where the time goes in v5:
time: 63.3 us; the launch traced here: 63.1 us
  Pallas kernels  58.5 us (92%)
  between operations  2.48 us (4%)
  other arithmetic  1.5 us (2%)
    pallas_call x1, Pallas kernels, per_device(): pl.pallas_call(list_kernel, out_shape=(shape((8, 4096), BF16), shape((1,)...  58.5 us
    broadcast_in_dim x1, other arithmetic, per_device(): return (loss, pooled_grad.astype(F32)[None], weight_grad)  1.5 us

profile of v5, /device:TPU:1, one launch (start us, length us, event | category | flops | bytes accessed | tf_op | source)
XLA Modules:
  0.0 63.1 jit_solution(7934167752159145881)
XLA Ops:
  0.6 58.5 %list.1 = (bf16[8,4096]{1,0:T(8,128)(2,1)}, f32[1]{0:T(128)}, f32[8,64]{1,0:T(8,128)}) custom-call(f32[64]{0:T(128)} %skip.1, bf16[128,4096]{1,0:T(8,128)(2,1)} %bitcast.15, bf16[128,128]{1,0:T(8,128)(2,1)} %bitcast.17, bf16[128,128]{1,0:T(8,128)(2,1)} %bitcast.18, f32[64,128]{1,0:T(8,128)} %bitcast.19, f32[64,128]{1,0:T(8,128)} %bitcast.20, ...), custom_call_target="tpu_custom_call" | custom-call | tf_op jit(solution)/shard_map/list/pallas_call | solution.py:470
  59.1 0.0 copy-start
  59.1 1.5 %bitcast_convert_fusion = f32[1,8,4096]{2,1,0:T(8,128)} fusion(bf16[8,4096]{1,0:T(8,128)(2,1)} %get-tuple-element.7), kind=kLoop, calls=%fused_computation | loop fusion | flops 32768 | bytes 196608 | tf_op jit(solution)/shard_map/broadcast_in_dim | solution.py:519
  61.3 0.0 copy-done
  61.3 0.6 copy.16
Async XLA Ops:
  59.1 2.2 %copy-start = (f32[8,64]{1,0:T(8,128)S(1)}, f32[8,64]{1,0:T(8,128)}, u32[]{:S(2)}) copy-start(f32[8,64]{1,0:T(8,128)} %get-tuple-element.14) | copy-start | bytes 6148

commit v6 on v5

--- a/solution.py
+++ b/solution.py
@@ -15,6 +15,7 @@
 CHIPS = 8
 AHEAD = 2
 MESH = pl.DeviceIdType.MESH
+NEAR_FIRST = sorted(range(1, NS), key=lambda k: min(k, NS - k))
 
 
 def dot(a, b, precision=None):
@@ -323,11 +324,8 @@
         rows = pl.ds(pl.multiple_of(peer(k) * 8, 8), 8)
         return exchange(margin_part.at[rows], r_margin.at[k], send_b.at[k], recv_b.at[k], k)
 
-    def start_b(k, _):
+    for k in reversed(NEAR_FIRST):
         margin_copy(k).start()
-        return 0
-
-    lax.fori_loop(1, NS, start_b, 0, unroll=True)
     r_margin[0] = margin_part[pl.ds(pl.multiple_of(me * 8, 8), 8), :]
     skew_rows = dot(pooled, skewed).astype(BF16)
     pooled_t = jnp.transpose(pooled.astype(F32)).astype(BF16)
@@ -337,11 +335,8 @@
     target = jnp.where(own_rank < ranks, 1.0, jnp.where(own_rank > ranks, 0.0, 0.5))
     valid = mask[...].astype(F32)
 
-    def wait_b(k, _):
-        margin_copy(k).wait()
-        return 0
-
-    lax.fori_loop(1, NS, wait_b, 0)
+    for k in NEAR_FIRST:
+        margin_copy(k).wait_recv()
     margin = jnp.sum(r_margin[...], axis=0)
     soft = jnp.maximum(margin, 0.0) + jnp.log(1.0 + jnp.exp(-jnp.abs(margin)))
     losses = jnp.sum(valid * (soft - target * margin), axis=0, keepdims=True)
@@ -355,19 +350,13 @@
     def pair_copy(k):
         return exchange(pair_own, r_pair.at[me], send_c.at[k], recv_c.at[k], k)
 
-    def start_c(k, _):
+    for k in reversed(NEAR_FIRST):
         pair_copy(k).start()
-        return 0
-
-    lax.fori_loop(1, NS, start_c, 0, unroll=True)
 
     pl.semaphore_wait(plane_sem, NS - 1)
 
-    def wait_c(k, _):
-        pair_copy(k).wait()
-        return 0
-
-    lax.fori_loop(1, NS, wait_c, 0)
+    for k in NEAR_FIRST:
+        pair_copy(k).wait_recv()
     pairs = r_pair[...].astype(F32)
     all_pair = pairs[:, :8, :].reshape(128, 128).astype(BF16)
     accumulated = dot(all_pair, pooled)
@@ -409,11 +398,8 @@
     def grad_copy(k):
         return exchange(grad_part.at[peer(k)], r_grad.at[me], send_d.at[k], recv_d.at[k], k)
 
-    def start_d(k, _):
+    for k in reversed(NEAR_FIRST):
         grad_copy(k).start()
-        return 0
-
-    lax.fori_loop(1, NS, start_d, 0, unroll=True)
     r_grad[me] = grad_part[me]
     loss_o[0] = jnp.sum(pairs[:, 8:10, :]) * (1.0 / (128.0 * 128.0))
 
@@ -427,25 +413,35 @@
 
     lax.fori_loop(0, CHIPS - 1, wait_a, 0)
 
-    def wait_d(k, _):
-        grad_copy(k).wait()
-        return 0
-
-    lax.fori_loop(1, NS, wait_d, 0)
+    for k in NEAR_FIRST:
+        grad_copy(k).wait_recv()
     for b in range(NS):
         pg_o[:, b * 256 : b * 256 + 256] = r_grad[b]
 
+    def wait_sent(k, _):
+        margin_copy(k).wait_send()
+        pair_copy(k).wait_send()
+        grad_copy(k).wait_send()
+        return 0
+
+    lax.fori_loop(1, NS, wait_sent, 0)
+
+    def wait_w_sent(i, _):
+        to_d, to_s, c = w_copy(i)
+
+        @pl.when(jnp.logical_not(jnp.logical_and(to_d == me_d, to_s == me)))
+        def _():
+            c.wait_send()
+
+        return 0
+
+    lax.fori_loop(0, ND, wait_w_sent, 0)
+
     def wait_w(i, _):
-        to_d, to_s, c = w_copy(i)
-
-        @pl.when(jnp.logical_not(jnp.logical_and(to_d == me_d, to_s == me)))
-        def _():
-            c.wait_send()
-
         arrived = pltpu.make_async_remote_copy(
             src_ref=w_part.at[0], dst_ref=r_w.at[i],
             send_sem=send_w.at[i], recv_sem=recv_w.at[i],
-            device_id=(to_d, to_s), device_id_type=MESH,
+            device_id=(me_d, peer(1)), device_id_type=MESH,
         )
 
         @pl.when(jnp.logical_or(i != me_d, home != me))
@@ -454,7 +450,7 @@
 
         return 0
 
-    lax.fori_loop(0, ND, wait_w, 0)
+    lax.fori_loop(0, ND, wait_w, 0, unroll=4)
     folded = jnp.sum(r_w[...].astype(F32), axis=0)
     wg_o[...] = jnp.concatenate([folded[:, :64], folded[:, 64:]], axis=0)
 

time: 63.3 us -> 62.6 us (0.989)
  Pallas kernels: 58.5 us -> 57.8 us
    pallas_call x1, Pallas kernels: 58.5 us -> 57.8 us  [per_device(): pl.pallas_call(list_kernel, out_shape=(shape((8, 4096), BF16), shape((1,)...]
where the time goes in v6:
time: 62.6 us; the launch traced here: 62.4 us
  Pallas kernels  57.8 us (92%)
  between operations  2.48 us (4%)
  other arithmetic  1.5 us (2%)
    pallas_call x1, Pallas kernels, per_device(): pl.pallas_call(list_kernel, out_shape=(shape((8, 4096), BF16), shape((1,)...  57.8 us
    broadcast_in_dim x1, other arithmetic, per_device(): return (loss, pooled_grad.astype(F32)[None], weight_grad)  1.5 us

profile of v6, /device:TPU:1, one launch (start us, length us, event | category | flops | bytes accessed | tf_op | source)
XLA Modules:
  0.0 62.4 jit_solution(3079330273844511606)
XLA Ops:
  0.6 57.8 %list.1 = (bf16[8,4096]{1,0:T(8,128)(2,1)}, f32[1]{0:T(128)}, f32[8,64]{1,0:T(8,128)}) custom-call(f32[64]{0:T(128)} %skip.1, bf16[128,4096]{1,0:T(8,128)(2,1)} %bitcast.15, bf16[128,128]{1,0:T(8,128)(2,1)} %bitcast.17, bf16[128,128]{1,0:T(8,128)(2,1)} %bitcast.18, f32[64,128]{1,0:T(8,128)} %bitcast.19, f32[64,128]{1,0:T(8,128)} %bitcast.20, ...), custom_call_target="tpu_custom_call" | custom-call | tf_op jit(solution)/shard_map/list/pallas_call | solution.py:466
  58.4 0.0 copy-start
  58.4 1.5 %bitcast_convert_fusion = f32[1,8,4096]{2,1,0:T(8,128)} fusion(bf16[8,4096]{1,0:T(8,128)(2,1)} %get-tuple-element.7), kind=kLoop, calls=%fused_computation | loop fusion | flops 32768 | bytes 196608 | tf_op jit(solution)/shard_map/broadcast_in_dim | solution.py:515
  60.6 0.0 copy-done
  60.6 0.6 copy.16
Async XLA Ops:
  58.4 2.2 %copy-start = (f32[8,64]{1,0:T(8,128)S(1)}, f32[8,64]{1,0:T(8,128)}, u32[]{:S(2)}) copy-start(f32[8,64]{1,0:T(8,128)} %get-tuple-element.14) | copy-start | bytes 6148
